TPU v7x, 32 devices: a whole 2x2x4 slice. The times are simulated.
32 devices in a mesh: fsdp: 8 (over z, y), tensor: 4 (over x, core).
Axes of the slice: x: 2, y: 2, z: 4, core: 2. Of those that a mesh axis runs over, the one named last changes fastest.
Arguments:
- block_input: bfloat16 [16, 197, 768], P('fsdp'), may hold values from -6 to 6
- output_grad: bfloat16 [16, 197, 768], P('fsdp'), may hold values from -6 to 6
- live_images: int32 [16], P('fsdp'), may hold values from 0 to 1, as said below
- w_qkv: float32 [768, 3, 768], P('fsdp', None, 'tensor'), may hold values from -6 to 6
- w_out: float32 [768, 768], P('tensor', 'fsdp'), may hold values from -0.625 to 0.625
- w_fc1: float32 [768, 3072], P('fsdp', 'tensor'), may hold values from -0.21875 to 0.21875
- w_fc2: float32 [3072, 768], P('tensor', 'fsdp'), may hold values from -0.109375 to 0.109375
- qv_bias: float32 [2, 12, 64], P(None, 'tensor', 'fsdp'), may hold values from -1.2 to 1.2
- fc1_bias: float32 [48, 64], P('tensor', 'fsdp'), may hold values from -1.2 to 1.2
- norm_vec: float32 [6, 768], P(None, 'fsdp'), may hold values from -0.9 to 1.5
- mom_qkv: float32 [2, 768, 3, 768], P(None, 'fsdp', None, 'tensor'), may hold values from -5.0528408 to 5.0528408, as said below
- mom_out: float32 [2, 768, 768], P(None, 'tensor', 'fsdp'), may hold values from -5.0528408 to 5.0528408, as said below
- mom_fc1: float32 [2, 768, 3072], P(None, 'fsdp', 'tensor'), may hold values from -5.0528408 to 5.0528408, as said below
- mom_fc2: float32 [2, 3072, 768], P(None, 'tensor', 'fsdp'), may hold values from -5.0528408 to 5.0528408, as said below
- mom_qvb: float32 [2, 2, 12, 64], P(None, None, 'tensor', 'fsdp'), may hold values from -5.0528408 to 5.0528408, as said below
- mom_fc1b: float32 [2, 48, 64], P(None, 'tensor', 'fsdp'), may hold values from -5.0528408 to 5.0528408, as said below
- mom_vec: float32 [2, 6, 768], P(None, None, 'fsdp'), may hold values from -5.0528408 to 5.0528408, as said below
Outputs:
- block_output: bfloat16 [16, 197, 768], P('fsdp')
- input_grad: float32 [16, 197, 768], P('fsdp')
- grad_qkv: float32 [768, 3, 768], P('fsdp', None, 'tensor')
- grad_out: float32 [768, 768], P('tensor', 'fsdp')
- grad_fc1: float32 [768, 3072], P('fsdp', 'tensor')
- grad_fc2: float32 [3072, 768], P('tensor', 'fsdp')
- grad_qvb: float32 [2, 12, 64], P(None, 'tensor', 'fsdp')
- grad_fc1b: float32 [48, 64], P('tensor', 'fsdp')
- grad_vec: float32 [6, 768], P(None, 'fsdp')
- new_qkv: float32 [768, 3, 768], P('fsdp', None, 'tensor')
- new_out: float32 [768, 768], P('tensor', 'fsdp')
- new_fc1: float32 [768, 3072], P('fsdp', 'tensor')
- new_fc2: float32 [3072, 768], P('tensor', 'fsdp')
- new_qvb: float32 [2, 12, 64], P(None, 'tensor', 'fsdp')
- new_fc1b: float32 [48, 64], P('tensor', 'fsdp')
- new_vec: float32 [6, 768], P(None, 'fsdp')
- newmom_qkv: float32 [2, 768, 3, 768], P(None, 'fsdp', None, 'tensor')
- newmom_out: float32 [2, 768, 768], P(None, 'tensor', 'fsdp')
- newmom_fc1: float32 [2, 768, 3072], P(None, 'fsdp', 'tensor')
- newmom_fc2: float32 [2, 3072, 768], P(None, 'tensor', 'fsdp')
- newmom_qvb: float32 [2, 2, 12, 64], P(None, None, 'tensor', 'fsdp')
- newmom_fc1b: float32 [2, 48, 64], P(None, 'tensor', 'fsdp')
- newmom_vec: float32 [2, 6, 768], P(None, None, 'fsdp')
Inputs may be any that keep to these rules, and one draw needn't show every extreme that they name: `live_images`: in each aligned block of 2 slots (those of one index of fsdp) either all images are live or exactly one slot is empty; blocks of both kinds occur in every draw. `mom_qkv`: the second moments are positive. `mom_out`: the second moments are positive. `mom_fc1`: the second moments are positive. `mom_fc2`: the second moments are positive. `mom_qvb`: the second moments are positive. `mom_fc1b`: the second moments are positive. `mom_vec`: the second moments are positive.
All inputs are finite; a program needn't handle non-finite values.
Results may differ from a plain program's by a relative error of at most 0.017.
Values may be sent and summed in bfloat16 or wider, within the bound.
A program may use at most 64 MiB of HBM per device.

v0:
```python
import functools

import jax
import jax.numpy as jnp
from jax import lax
from jax.experimental import pallas as pl
from jax.experimental.pallas import tpu as pltpu
from jax.sharding import PartitionSpec as P

HD = 64


epsilon = 1e-06
sqrt_half = 0.7071067811865476
inv_root = 0.3989422804014327
corr_one = 1.0 - 0.9**3
corr_two = 1.0 - 0.999**3


def norm_forward(values, gain, shift):
    center = values - jnp.mean(values, axis=-1, keepdims=True)
    variance = jnp.mean(center * center, axis=-1, keepdims=True)
    scale = lax.rsqrt(variance + epsilon)
    normed = center * scale
    return (normed * gain + shift, normed, scale)


def norm_backward(upstream, normed, scale, gain):
    scaled = upstream * gain
    return scale * (
        scaled
        - jnp.mean(scaled, axis=-1, keepdims=True)
        - normed * jnp.mean(scaled * normed, axis=-1, keepdims=True)
    )


def gelu_slope(pre_act):
    return (
        0.5 * (1.0 + lax.erf(pre_act * sqrt_half))
        + pre_act * jnp.exp(-0.5 * pre_act * pre_act) * inv_root
    )


def attend(queries, key_rows, value_rows):
    scores = (
        jnp.einsum("bqhe,bkhe->bhqk", queries, key_rows, preferred_element_type=jnp.float32) * 0.125
    )
    logsum = jax.nn.logsumexp(scores, axis=-1, keepdims=True)
    probs = jnp.exp(scores - logsum).astype(jnp.bfloat16)
    mixed = jnp.einsum("bhqk,bkhe->bqhe", probs, value_rows, preferred_element_type=jnp.float32)
    return (mixed.astype(jnp.bfloat16), logsum)


def attend_back(queries, key_rows, value_rows, logsum, upstream):
    scores = (
        jnp.einsum("bqhe,bkhe->bhqk", queries, key_rows, preferred_element_type=jnp.float32) * 0.125
    )
    probs = jnp.exp(scores - logsum)
    probs_low = probs.astype(jnp.bfloat16)
    dprobs = jnp.einsum("bqhe,bkhe->bhqk", upstream, value_rows, preferred_element_type=jnp.float32)
    dscore = (probs * (dprobs - jnp.sum(probs * dprobs, axis=-1, keepdims=True))).astype(
        jnp.bfloat16
    )
    dquery = 0.125 * jnp.einsum(
        "bhqk,bkhe->bqhe", dscore, key_rows, preferred_element_type=jnp.float32
    )
    dkey = 0.125 * jnp.einsum(
        "bhqk,bqhe->bkhe", dscore, queries, preferred_element_type=jnp.float32
    )
    dvalue = jnp.einsum("bhqk,bqhe->bkhe", probs_low, upstream, preferred_element_type=jnp.float32)
    return (dquery, dkey, dvalue)


def adamw(param, grad, moments):
    first = 0.9 * moments[0] + 0.1 * grad
    second = 0.999 * moments[1] + 0.001 * grad * grad
    fresh = param - 0.004 * (
        first / corr_one / (jnp.sqrt(second / corr_two) + 1e-08) + 0.05 * param
    )
    return (fresh, jnp.stack([first, second]))


MESH_ID = pl.DeviceIdType.MESH


def exchange(fsdp, tensor, tag, gathers=(), reduces=(), terms=()):
    far_n, across_n = fsdp // 2, tensor // 2
    n_g, n_r, n_t = len(gathers), len(reduces), len(terms)
    low = jnp.bfloat16

    def kernel(*refs):
        refs = list(refs)

        def take(count):
            out, refs[:] = refs[:count], refs[count:]
            return out

        g_in, r_in, t_in = take(n_g), take(n_r), take(n_t)
        g_out, r_out, t_out = take(n_g), take(n_r), take(n_t)
        r_near, r_sum, r_far = take(n_r), take(n_r), take(n_r)
        t_core, t_half, t_across = take(n_t), take(n_t), take(n_t)
        g_send, g_recv, r_send, r_recv, t_send, t_recv = take(6)
        mine = lax.axis_index("fsdp")
        lane = lax.axis_index("tensor")
        far, near = lax.div(mine, 2), lax.rem(mine, 2)
        across, core = lax.div(lane, 2), lax.rem(lane, 2)
        twin = 2 * far + (1 - near)
        mate = 2 * across + (1 - core)

        def ahead(step):
            return lax.rem(far + step, far_n)

        def behind(step):
            return lax.rem(far + far_n - step, far_n)

        barrier = pltpu.get_barrier_semaphore()
        greeted = 0
        if n_g or n_r:
            for who in [twin] + [2 * ahead(j) + near for j in range(1, far_n)]:
                pl.semaphore_signal(barrier, inc=1, device_id=(who, lane), device_id_type=MESH_ID)
                greeted += 1
        if n_t:
            for who in [mate] + [
                2 * lax.rem(across + j, across_n) + core for j in range(1, across_n)
            ]:
                pl.semaphore_signal(barrier, inc=1, device_id=(mine, who), device_id_type=MESH_ID)
                greeted += 1
        pl.semaphore_wait(barrier, greeted)

        def copy(src, dst, send, recv, target):
            return pltpu.make_async_remote_copy(
                src_ref=src,
                dst_ref=dst,
                send_sem=send,
                recv_sem=recv,
                device_id=target,
                device_id_type=MESH_ID,
            )

        def run_gather():
            sent = []
            for j in range(1, far_n):
                for p in range(n_g):
                    sent.append(
                        copy(g_in[p], g_out[p].at[mine], g_send.at[p, j], g_recv.at[p, j],
                             (2 * ahead(j) + near, lane))
                    )
                    sent[-1].start()
            for p in range(n_g):
                sent.append(
                    copy(g_in[p], g_out[p].at[mine], g_send.at[p, far_n], g_recv.at[p, far_n],
                         (twin, lane))
                )
                sent[-1].start()
                g_out[p][mine] = g_in[p][...]
            yield
            for j in range(1, far_n):
                for p in range(n_g):
                    slot = g_out[p].at[2 * behind(j) + near]
                    copy(g_in[p], slot, g_send.at[p, j], g_recv.at[p, j],
                         (2 * ahead(j) + near, lane)).wait_recv()
                    sent.append(
                        copy(slot, slot, g_send.at[p, far_n + j], g_recv.at[p, far_n + j],
                             (twin, lane))
                    )
                    sent[-1].start()
                yield
            for j in range(far_n):
                for p in range(n_g):
                    slot = g_out[p].at[2 * behind(j) + (1 - near)]
                    copy(g_in[p], slot, g_send.at[p, far_n + j], g_recv.at[p, far_n + j],
                         (twin, lane)).wait_recv()
            for entry in sent:
                entry.wait_send()

        def run_reduce():
            order = list(range(1, far_n)) + [0]
            hops = {}
            for p in range(n_r):
                for j in order:
                    hops[p, j] = copy(
                        r_in[p].at[2 * ahead(j) + (1 - near)], r_near[p].at[j],
                        r_send.at[p, j], r_recv.at[p, j], (twin, lane))
                    hops[p, j].start()
            yield
            sent = {}
            for p in range(n_r):
                for j in range(1, far_n):
                    hops[p, j].wait_recv()
                    total = r_in[p][2 * ahead(j) + near].astype(jnp.float32) + r_near[p][j].astype(
                        jnp.float32
                    )
                    r_sum[p][j - 1] = total.astype(r_sum[p].dtype)
                    sent[p, j] = copy(
                        r_sum[p].at[j - 1], r_far[p].at[j - 1],
                        r_send.at[p, far_n + j], r_recv.at[p, far_n + j],
                        (2 * ahead(j) + near, lane))
                    sent[p, j].start()
                    yield
            for p in range(n_r):
                hops[p, 0].wait_recv()
                total = r_in[p][mine].astype(jnp.float32) + r_near[p][0].astype(jnp.float32)
                for j in range(1, far_n):
                    sent[p, j].wait_recv()
                    total = total + r_far[p][j - 1].astype(jnp.float32)
                r_out[p][...] = total
            for entry in list(hops.values()) + list(sent.values()):
                entry.wait_send()

        def run_terms():
            half = [ref.shape[1] // 2 for ref in t_in]
            own = [pl.ds(pl.multiple_of(core * h, h), h) for h in half]
            other = [pl.ds(pl.multiple_of((1 - core) * h, h), h) for h in half]
            first, second, third = {}, {}, {}
            for p in range(n_t):
                first[p] = copy(t_in[p].at[:, other[p]], t_core[p], t_send.at[p, 0],
                                t_recv.at[p, 0], (mine, mate))
                first[p].start()
            yield
            for p in range(n_t):
                first[p].wait_recv()
                t_half[p][...] = (
                    t_in[p][:, own[p]].astype(jnp.float32) + t_core[p][...].astype(jnp.float32)
                ).astype(low)
                for j in range(1, across_n):
                    second[p, j] = copy(
                        t_half[p], t_across[p].at[j - 1], t_send.at[p, 1 + j], t_recv.at[p, 1 + j],
                        (mine, 2 * lax.rem(across + j, across_n) + core))
                    second[p, j].start()
            yield
            yield
            for p in range(n_t):
                total = t_half[p][...].astype(jnp.float32)
                for j in range(1, across_n):
                    second[p, j].wait_recv()
                    total = total + t_across[p][j - 1].astype(jnp.float32)
                t_out[p][:, own[p]] = total.astype(low)
                third[p] = copy(t_out[p].at[:, own[p]], t_out[p].at[:, own[p]], t_send.at[p, 1],
                                t_recv.at[p, 1], (mine, mate))
                third[p].start()
            yield
            for p in range(n_t):
                copy(t_out[p].at[:, own[p]], t_out[p].at[:, other[p]], t_send.at[p, 1],
                     t_recv.at[p, 1], (mine, mate)).wait_recv()
            for entry in list(first.values()) + list(second.values()) + list(third.values()):
                entry.wait_send()

        flows = []
        if n_t:
            flows.append(run_terms())
        if n_g:
            flows.append(run_gather())
        if n_r:
            flows.append(run_reduce())
        while flows:
            for flow in list(flows):
                if next(flow, "end") == "end":
                    flows.remove(flow)

    shape = jax.ShapeDtypeStruct
    outs = (
        [shape((fsdp,) + a.shape, a.dtype) for a in gathers]
        + [shape(a.shape[1:], jnp.float32) for a in reduces]
        + [shape(a.shape, a.dtype) for a in terms]
    )
    few = max(far_n - 1, 1)
    scratch = (
        [pltpu.VMEM((far_n,) + a.shape[1:], a.dtype) for a in reduces]
        + [pltpu.VMEM((few,) + a.shape[1:], a.dtype) for a in reduces]
        + [pltpu.VMEM((few,) + a.shape[1:], a.dtype) for a in reduces]
        + [pltpu.VMEM((a.shape[0], a.shape[1] // 2), low) for a in terms]
        + [pltpu.VMEM((a.shape[0], a.shape[1] // 2), low) for a in terms]
        + [pltpu.VMEM((max(across_n - 1, 1), a.shape[0], a.shape[1] // 2), low) for a in terms]
        + [pltpu.SemaphoreType.DMA((max(n_g, 1), 2 * far_n))] * 2
        + [pltpu.SemaphoreType.DMA((max(n_r, 1), 2 * far_n))] * 2
        + [pltpu.SemaphoreType.DMA((max(n_t, 1), 1 + across_n))] * 2
    )
    args = tuple(gathers) + tuple(reduces) + tuple(terms)
    return pl.pallas_call(
        kernel,
        out_shape=tuple(outs),
        in_specs=[pl.BlockSpec(memory_space=pltpu.VMEM)] * len(args),
        out_specs=tuple([pl.BlockSpec(memory_space=pltpu.VMEM)] * len(outs)),
        scratch_shapes=scratch,
        compiler_params=pltpu.CompilerParams(
            collective_id=tag, has_side_effects=True, vmem_limit_bytes=48 * 1024 * 1024
        ),
        name="exchange_" + str(tag),
    )(*args)


def row_of(values, lanes):
    return jnp.pad(values, [(0, 0)] * (values.ndim - 1) + [(0, lanes - values.shape[-1])])


def on_device(
    fsdp,
    tensor,
    block_input,
    output_grad,
    live_images,
    w_qkv,
    w_out,
    w_fc1,
    w_fc2,
    qv_bias,
    fc1_bias,
    norm_vec,
    mom_qkv,
    mom_out,
    mom_fc1,
    mom_fc2,
    mom_qvb,
    mom_fc1b,
    mom_vec,
):
    low = jnp.bfloat16
    images, seqlen, width = block_input.shape
    rows = images * seqlen
    owned_rows, _, local_feat = w_qkv.shape
    hidden = w_fc1.shape[1]
    heads_here = local_feat // HD
    n_qvb, n_fc1b = qv_bias.size, fc1_bias.size
    vec_rows = norm_vec.shape[0]
    lanes = -(-max(owned_rows, n_qvb, n_fc1b) // 128) * 128
    small_rows = 16

    small = jnp.concatenate(
        [
            row_of(norm_vec, lanes),
            row_of(fc1_bias.reshape(1, n_fc1b), lanes),
            row_of(qv_bias.reshape(1, n_qvb), lanes),
            jnp.zeros((small_rows - vec_rows - 2, lanes), jnp.float32),
        ]
    ).astype(low)
    small_all, inward, outward = exchange(
        fsdp,
        tensor,
        1,
        gathers=(
            small,
            w_qkv.astype(low).reshape(owned_rows, 3 * local_feat),
            w_out.astype(low).T,
        ),
    )
    inward = inward.reshape(width, 3 * local_feat)
    outward = outward.reshape(width, local_feat)
    smallf = small_all.astype(jnp.float32)
    vecf = smallf[:, :vec_rows, :owned_rows].transpose(1, 0, 2).reshape(vec_rows, width)
    hidden_bias = (
        smallf[:, vec_rows, :n_fc1b]
        .reshape((fsdp,) + fc1_bias.shape)
        .transpose(1, 0, 2)
        .reshape(hidden)
    )
    biasf = (
        smallf[:, vec_rows + 1, :n_qvb]
        .reshape((fsdp,) + qv_bias.shape)
        .transpose(1, 2, 0, 3)
        .reshape(2, local_feat)
    )
    flat = block_input.astype(jnp.float32).reshape(rows, width)
    first_norm, unit_one, scale_one = norm_forward(flat, vecf[0], vecf[1])
    normed_one = first_norm.astype(low)
    shifts = jnp.concatenate([biasf[0], jnp.zeros_like(biasf[0]), biasf[1]])
    projected = jnp.dot(normed_one, inward, preferred_element_type=jnp.float32) + shifts
    triple = projected.astype(low).reshape(images, seqlen, 3, heads_here, HD)
    queries = triple[:, :, 0]
    key_rows = triple[:, :, 1]
    value_rows = triple[:, :, 2]
    mixed, logsum = attend(queries, key_rows, value_rows)
    attn_rows = mixed.reshape(rows, local_feat)
    attn_term = jnp.einsum(
        "nj,dj->nd", attn_rows, outward, preferred_element_type=jnp.float32
    ).astype(low)
    widen, narrow, attn_total = exchange(
        fsdp,
        tensor,
        2,
        gathers=(w_fc1.astype(low), w_fc2.astype(low).T),
        terms=(attn_term,),
    )
    widen = widen.reshape(width, hidden)
    narrow = narrow.reshape(width, hidden)
    resid = flat + attn_total.astype(jnp.float32) + vecf[4]
    second_norm, unit_two, scale_two = norm_forward(resid, vecf[2], vecf[3])
    normed_two = second_norm.astype(low)
    pre_act = jnp.dot(normed_two, widen, preferred_element_type=jnp.float32) + hidden_bias
    activ = jax.nn.gelu(pre_act, approximate=False).astype(low)
    mlp_term = jnp.einsum(
        "nf,df->nd", activ, narrow, preferred_element_type=jnp.float32
    ).astype(low)
    row_mask = jnp.broadcast_to(live_images.astype(jnp.float32)[:, None], (images, seqlen)).reshape(
        rows, 1
    )
    grad_flat = output_grad.astype(jnp.float32).reshape(rows, width) * row_mask
    grad_low = grad_flat.astype(low)
    grad_narrow = jnp.einsum("nd,nf->df", grad_low, activ, preferred_element_type=jnp.float32)
    delta_act = jnp.einsum("nd,df->nf", grad_low, narrow, preferred_element_type=jnp.float32)
    delta_pre = delta_act * gelu_slope(pre_act)
    delta_pre_low = delta_pre.astype(low)
    grad_hidden = jnp.sum(delta_pre, axis=0)
    grad_widen = jnp.einsum(
        "nd,nf->df", normed_two, delta_pre_low, preferred_element_type=jnp.float32
    )
    two_term = jnp.einsum(
        "nf,df->nd", delta_pre_low, widen, preferred_element_type=jnp.float32
    ).astype(low)

    def blocks(grad):
        return grad.astype(low).reshape(fsdp, owned_rows, grad.shape[1])

    own_narrow, own_widen, delta_two, mlp_total = exchange(
        fsdp,
        tensor,
        3,
        reduces=(blocks(grad_narrow), blocks(grad_widen)),
        terms=(two_term, mlp_term),
    )
    delta_two = delta_two.astype(jnp.float32)
    block_output = (
        (row_mask * (resid + mlp_total.astype(jnp.float32) + vecf[5]))
        .astype(low)
        .reshape(images, seqlen, width)
    )
    delta_resid = grad_flat + norm_backward(delta_two, unit_two, scale_two, vecf[2])
    delta_resid_low = delta_resid.astype(low)
    grad_outward = jnp.einsum(
        "nd,nj->dj", delta_resid_low, attn_rows, preferred_element_type=jnp.float32
    )
    delta_mixed = jnp.dot(delta_resid_low, outward, preferred_element_type=jnp.float32)
    delta_mixed = delta_mixed.astype(low).reshape(images, seqlen, heads_here, HD)
    delta_query, delta_key, delta_value = attend_back(
        queries, key_rows, value_rows, logsum, delta_mixed
    )
    delta_triple = jnp.stack([delta_query, delta_key, delta_value], axis=2).reshape(
        rows, 3 * local_feat
    )
    grad_heads = jnp.stack(
        [
            jnp.sum(delta_query, axis=(0, 1)).reshape(local_feat),
            jnp.sum(delta_value, axis=(0, 1)).reshape(local_feat),
        ]
    )
    triple_low = delta_triple.astype(low)
    grad_inward = jnp.einsum(
        "nd,nj->dj", normed_one, triple_low, preferred_element_type=jnp.float32
    )
    one_term = jnp.einsum(
        "nj,dj->nd", triple_low, inward, preferred_element_type=jnp.float32
    ).astype(low)
    own_inward, own_outward, delta_one = exchange(
        fsdp,
        tensor,
        4,
        reduces=(blocks(grad_inward), blocks(grad_outward)),
        terms=(one_term,),
    )
    delta_one = delta_one.astype(jnp.float32)
    input_grad = (delta_resid + norm_backward(delta_one, unit_one, scale_one, vecf[0])).reshape(
        images, seqlen, width
    )
    grad_rows_vec = jnp.stack(
        [
            jnp.sum(delta_one * unit_one, axis=0),
            jnp.sum(delta_one, axis=0),
            jnp.sum(delta_two * unit_two, axis=0),
            jnp.sum(delta_two, axis=0),
            jnp.sum(delta_resid, axis=0),
            jnp.sum(grad_flat, axis=0),
        ]
    )
    r_fc1b, c_fc1b = fc1_bias.shape
    k_qvb, r_qvb, c_qvb = qv_bias.shape
    small_grads = jnp.concatenate(
        [
            row_of(grad_rows_vec.reshape(vec_rows, fsdp, owned_rows).transpose(1, 0, 2), lanes),
            row_of(
                grad_hidden.reshape(r_fc1b, fsdp, c_fc1b).transpose(1, 0, 2).reshape(
                    fsdp, 1, n_fc1b
                ),
                lanes,
            ),
            row_of(
                grad_heads.reshape(k_qvb, r_qvb, fsdp, c_qvb).transpose(2, 0, 1, 3).reshape(
                    fsdp, 1, n_qvb
                ),
                lanes,
            ),
        ],
        axis=1,
    )
    (own_small,) = exchange(fsdp, tensor, 5, reduces=(small_grads,))
    owned = (
        own_inward.reshape(w_qkv.shape),
        own_outward.T,
        own_widen,
        own_narrow.T,
        own_small[vec_rows + 1, :n_qvb].reshape(qv_bias.shape),
        own_small[vec_rows, :n_fc1b].reshape(fc1_bias.shape),
        own_small[:vec_rows, :owned_rows],
    )
    params = (w_qkv, w_out, w_fc1, w_fc2, qv_bias, fc1_bias, norm_vec)
    moments = (mom_qkv, mom_out, mom_fc1, mom_fc2, mom_qvb, mom_fc1b, mom_vec)
    stepped = [adamw(param, grad, moment) for param, grad, moment in zip(params, owned, moments)]
    return (
        (block_output, input_grad)
        + tuple(owned)
        + tuple((entry[0] for entry in stepped))
        + tuple((entry[1] for entry in stepped))
    )


def solution(mesh):
    return jax.shard_map(
        functools.partial(on_device, mesh.shape["fsdp"], mesh.shape["tensor"]),
        mesh=mesh,
        in_specs=(
            P("fsdp", None, None),
            P("fsdp", None, None),
            P("fsdp"),
            P("fsdp", None, "tensor"),
            P("tensor", "fsdp"),
            P("fsdp", "tensor"),
            P("tensor", "fsdp"),
            P(None, "tensor", "fsdp"),
            P("tensor", "fsdp"),
            P(None, "fsdp"),
            P(None, "fsdp", None, "tensor"),
            P(None, "tensor", "fsdp"),
            P(None, "fsdp", "tensor"),
            P(None, "tensor", "fsdp"),
            P(None, None, "tensor", "fsdp"),
            P(None, "tensor", "fsdp"),
            P(None, None, "fsdp"),
        ),
        out_specs=(
            P("fsdp", None, None),
            P("fsdp", None, None),
            P("fsdp", None, "tensor"),
            P("tensor", "fsdp"),
            P("fsdp", "tensor"),
            P("tensor", "fsdp"),
            P(None, "tensor", "fsdp"),
            P("tensor", "fsdp"),
            P(None, "fsdp"),
            P("fsdp", None, "tensor"),
            P("tensor", "fsdp"),
            P("fsdp", "tensor"),
            P("tensor", "fsdp"),
            P(None, "tensor", "fsdp"),
            P("tensor", "fsdp"),
            P(None, "fsdp"),
            P(None, "fsdp", None, "tensor"),
            P(None, "tensor", "fsdp"),
            P(None, "fsdp", "tensor"),
            P(None, "tensor", "fsdp"),
            P(None, None, "tensor", "fsdp"),
            P(None, "tensor", "fsdp"),
            P(None, None, "fsdp"),
        ),
        check_vma=False,
    )
```

profile of v0, /device:TPU:0, one launch (start us, length us, event | category | flops | bytes accessed | tf_op | source)
XLA Modules:
  0.0 232.8 jit_solution(6414826665010993136)
XLA Ops:
  3.6 26.8 %exchange_1.1 = (bf16[8,16,128]{2,1,0:T(8,128)(2,1)S(1)}, bf16[8,96,576]{2,1,0:T(8,128)(2,1)S(1)}, bf16[8,96,192]{2,1,0:T(8,128)(2,1)S(1)}) custom-call(bf16[16,128]{1,0:T(8,128)(2,1)S(1)} %fusion.94.refs_0_, bf16[96,576]{1,0:T(8,128)(2,1)S(1)} %copy.251.refs_1_, bf16[96,192]{1,0:T(8,128)(2,1)S(1)} %convert_bitcast_fusion.3.refs_2_), custom_call_target="tpu_custom_call" | custom-call | tf_op jit(solution)/shard_map/exchange_1/pallas_call | solution.py:279
  33.2 1.4 add_convert_fusion.1
  36.0 1.7 fusion.6
  45.5 33.9 %exchange_2.1 = (bf16[8,96,768]{2,1,0:T(8,128)(2,1)S(1)}, bf16[8,96,768]{2,1,0:T(8,128)(2,1)S(1)}, bf16[394,768]{1,0:T(8,128)(2,1)S(1)}) custom-call(bf16[96,768]{1,0:T(8,128)(2,1)S(1)} %convert_element_type.138.refs_0_, bf16[96,768]{1,0:T(8,128)(2,1)S(1)} %convert_bitcast_fusion.2.refs_1_, bf16[394,768]{1,0:T(8,128)(2,1)S(1)} %convolution_convert_fusion.6.refs_2_), custom_call_target="tpu_custom_call" | custom-call | tf_op jit(solution)/shard_map/exchange_2/pallas_call | solution.py:279
  81.7 1.4 reshape.414
  85.9 5.6 %fusion.17 = (bf16[394,768]{1,0:T(8,128)(2,1)S(1)}, f32[394,768]{1,0:T(8,128)}) fusion(f32[768]{0:T(1024)S(1)} %add.254, bf16[768,768]{1,0:T(8,128)(2,1)S(1)} %bitcast.211, f32[394,768]{1,0:T(8,128)} %copy-done.12, f32[768]{0:T(1024)S(1)} %add.251, f32[768]{0:T(1024)S(1)} %mul.612, f32[394]{0:T(512)S(1)} %add_rsqrt_fusion.1, ...), kind=kOutput, calls=%fused_computation.36 | convolution fusion | flops 486265344 | bytes 4217936 | tf_op jit(solution)/shard_map/dot_general | solution.py:388
  94.8 2.7 %fusion.115 = (f32[768]{0:T(1024)S(1)}, bf16[394,768]{1,0:T(8,128)(2,1)S(1)}) fusion(f32[394,768]{1,0:T(8,128)} %get-tuple-element.205, bf16[394,768]{1,0:T(8,128)(2,1)} %convert_element_type.157, bf16[768,768]{1,0:T(8,128)(2,1)} %bitcast.213), kind=kOutput, calls=%fused_computation.241 | convolution fusion | flops 468109056 | bytes 3603456 | tf_op jit(solution)/shard_map/nd,df->nf/dot_general | solution.py:399
  97.5 1.5 convolution_convert_fusion.5.refs_2_
  101.6 2.5 %reshape.422 = f32[394,768]{1,0:T(8,128)} reshape(f32[2,197,768]{2,1,0:T(8,128)} %copy.261) | data formatting | bytes 2420736 | tf_op jit(solution)/shard_map/reshape | solution.py:396
  104.1 2.2 convolution_convert_fusion.1
  106.4 40.0 %exchange_3.1 = (f32[96,768]{1,0:T(8,128)S(1)}, f32[96,768]{1,0:T(8,128)S(1)}, bf16[394,768]{1,0:T(8,128)(2,1)S(1)}, bf16[394,768]{1,0:T(8,128)(2,1)S(1)}) custom-call(bf16[8,96,768]{2,1,0:T(8,128)(2,1)S(1)} %bitcast.208, bf16[8,96,768]{2,1,0:T(8,128)(2,1)S(1)} %bitcast.207, bf16[394,768]{1,0:T(8,128)(2,1)S(1)} %copy-done, ...), custom_call_target="tpu_custom_call" | custom-call | tf_op jit(solution)/shard_map/exchange_3/pallas_call | solution.py:279
  148.3 3.6 %fusion.103 = (f32[768]{0:T(1024)S(1)}, f32[394,768]{1,0:T(8,128)}, bf16[394,768]{1,0:T(8,128)(2,1)}) fusion(f32[394]{0:T(512)S(1)} %broadcast_multiply_fusion.3, f32[394,768]{1,0:T(8,128)} %copy-done.12, f32[394]{0:T(512)S(1)} %broadcast_multiply_fusion.5, f32[394]{0:T(512)S(1)} %broadcast_multiply_fusion.4, f32[768]{0:T(1024)S(1)} %mul.612, ...), kind=kLoop, calls=%fused_computation.230 | loop fusion | flops 4840704 | bytes 5463752 | tf_op jit(solution)/shard_map/reduce_sum | solution.py:469
  151.9 1.7 convolution_convert_fusion.9
  153.8 1.8 multiply_reduce_fusion
  159.5 1.9 convolution_convert_fusion.3.refs_2_
  161.3 1.7 convolution_convert_fusion.7
  163.2 2.6 %convolution_convert_fusion.2 = bf16[768,576]{0,1:T(8,128)(2,1)} fusion(bf16[394,768]{1,0:T(8,128)(2,1)S(1)} %copy-done.34, bf16[394,576]{0,1:T(8,128)(2,1)} %convert_element_type.168), kind=kOutput, calls=%fused_computation.16 | convolution fusion | flops 349028352 | bytes 1943808 | tf_op jit(solution)/shard_map/nd,nj->dj/dot_general | solution.py:446
  165.8 1.8 copy.270
  167.6 26.1 %exchange_4.1 = (f32[96,576]{1,0:T(8,128)S(1)}, f32[96,192]{1,0:T(8,128)S(1)}, bf16[394,768]{1,0:T(8,128)(2,1)S(1)}) custom-call(bf16[8,96,576]{2,1,0:T(8,128)(2,1)S(1)} %bitcast.203, bf16[8,96,192]{2,1,0:T(8,128)(2,1)S(1)} %bitcast.206, bf16[394,768]{1,0:T(8,128)(2,1)S(1)} %convolution_convert_fusion.3.refs_2_), custom_call_target="tpu_custom_call" | custom-call | tf_op jit(solution)/shard_map/exchange_4/pallas_call | solution.py:279
  195.7 2.0 fusion.23
  198.7 8.9 %exchange_5.1 = f32[8,128]{1,0:T(8,128)S(1)} custom-call(f32[8,8,128]{2,1,0:T(8,128)S(1)} %select_maximum_fusion.refs_0_), custom_call_target="tpu_custom_call" | custom-call | tf_op jit(solution)/shard_map/exchange_5/pallas_call | solution.py:279
  220.2 3.1 %fusion.9 = f32[394,768]{1,0:T(8,128)} fusion(f32[394,768]{1,0:T(8,128)} %get-tuple-element.158, bf16[394,768]{1,0:T(8,128)(2,1)S(1)} %get-tuple-element.44, f32[394,768]{1,0:T(8,128)} %copy-done.11, f32[394]{0:T(512)S(1)} %broadcast_multiply_fusion.1, f32[394]{0:T(512)S(1)} %div.138, f32[394]{0:T(512)S(1)} %broadcast_multiply_fusion.2, f32[768]{0:T(1024)S(1)} %mul.604, ...), kind=kLoop, calls=%fused_computation.28 | loop fusion | flops 2723328 | bytes 4245664 | tf_op jit(solution)/shard_map/add | solution.py:460
  223.3 1.4 reshape.431
  224.7 1.6 copy.303
  (266 shorter events, 53.1 us)
Async XLA Ops:
  0.7 2.5 %copy-start.41 = (f32[12,8]{0,1:T(8,128)S(1)}, f32[12,8]{0,1:T(8,128)}, u32[]{:S(2)}) copy-start(f32[12,8]{0,1:T(8,128)} %param.25) | copy-start | bytes 1156
  0.7 2.7 %copy-start.46 = (f32[2,3,8]{2,0,1:T(2,128)S(1)}, f32[2,3,8]{2,0,1:T(2,128)}, u32[]{:S(2)}) copy-start(f32[2,3,8]{2,0,1:T(2,128)} %param.24) | copy-start | bytes 580
  0.7 2.8 %copy-start.43 = (f32[6,96]{1,0:T(8,128)S(1)}, f32[6,96]{1,0:T(8,128)}, u32[]{:S(2)}) copy-start(f32[6,96]{1,0:T(8,128)} %param.26) | copy-start | bytes 6916
  0.7 30.7 %copy-start.15 = (bf16[2,197,768]{2,0,1:T(2,128)(2,1)S(1)}, bf16[2,197,768]{2,0,1:T(2,128)(2,1)}, u32[]{:S(2)}) copy-start(bf16[2,197,768]{2,0,1:T(2,128)(2,1)} %param.17) | copy-start | bytes 1815556
  30.4 5.6 %copy-start.7 = (bf16[8,96,576]{2,1,0:T(8,128)(2,1)}, bf16[8,96,576]{2,1,0:T(8,128)(2,1)S(1)}, u32[]{:S(2)}) copy-start(bf16[8,96,576]{2,1,0:T(8,128)(2,1)S(1)} %get-tuple-element.37) | copy-start | bytes 2654212
  30.5 5.2 %copy-start.38 = (f32[8,16,128]{2,1,0:T(8,128)}, f32[8,16,128]{2,1,0:T(8,128)S(1)}, u32[]{:S(2)}) copy-start(f32[8,16,128]{2,1,0:T(8,128)S(1)} %convert_element_type.142) | copy-start | bytes 196612
  40.9 1.9 copy-start.25
  42.6 1.9 copy-start.9
  83.1 8.4 %copy-start.11 = (f32[394,768]{1,0:T(8,128)}, f32[394,768]{1,0:T(8,128)S(1)}, u32[]{:S(2)}) copy-start(f32[394,768]{1,0:T(8,128)S(1)} %reshape.414) | copy-start | bytes 3631108
  84.9 6.6 %copy-start.50 = (f32[768]{0:T(1024)}, f32[768]{0:T(1024)S(1)}, u32[]{:S(2)}) copy-start(f32[768]{0:T(1024)S(1)} %add.251) | copy-start | bytes 9220
  85.9 5.6 %copy-start.6 = (bf16[8,96,768]{2,1,0:T(8,128)(2,1)S(1)}, bf16[8,96,768]{2,1,0:T(8,128)(2,1)}, u32[]{:S(2)}) copy-start(bf16[8,96,768]{2,1,0:T(8,128)(2,1)} %copy-done.5) | copy-start | bytes 3538948
  101.6 2.5 %copy-start.54 = (bf16[394,768]{1,0:T(8,128)(2,1)S(1)}, bf16[394,768]{1,0:T(8,128)(2,1)}, u32[]{:S(2)}) copy-start(bf16[394,768]{1,0:T(8,128)(2,1)} %copy-done.53) | copy-start | bytes 1815556
  104.1 2.3 copy-start
  106.4 40.9 %copy-start.14 = (f32[394,768]{1,0:T(8,128)S(1)}, f32[394,768]{1,0:T(8,128)}, u32[]{:S(2)}) copy-start(f32[394,768]{1,0:T(8,128)} %copy-done.12) | copy-start | bytes 3631108
  151.9 1.9 copy-start.22
  195.6 12.0 %copy-start.48 = (f32[2,6,96]{2,0,1:T(2,128)S(1)}, f32[2,6,96]{2,0,1:T(2,128)}, u32[]{:S(2)}) copy-start(f32[2,6,96]{2,0,1:T(2,128)} %param.33) | copy-start | bytes 13828
  195.6 12.1 %copy-start.44 = (f32[6,96]{1,0:T(8,128)S(1)}, f32[6,96]{1,0:T(8,128)}, u32[]{:S(2)}) copy-start(f32[6,96]{1,0:T(8,128)} %param.26) | copy-start | bytes 6916
  195.6 13.5 %copy-start.39 = (f32[2,12,8]{1,2,0:T(8,128)S(1)}, f32[2,12,8]{1,2,0:T(8,128)}, u32[]{:S(2)}) copy-start(f32[2,12,8]{1,2,0:T(8,128)} %param.32) | copy-start | bytes 2308
  195.6 14.2 %copy-start.49 = (f32[2,2,3,8]{3,1,2,0:T(2,128)S(1)}, f32[2,2,3,8]{3,1,2,0:T(2,128)}, u32[]{:S(2)}) copy-start(f32[2,2,3,8]{3,1,2,0:T(2,128)} %param.31) | copy-start | bytes 1156
  195.6 14.8 %copy-start.29 = (f32[768,96]{0,1:T(8,128)S(1)}, f32[768,96]{0,1:T(8,128)}, u32[]{:S(2)}) copy-start(f32[768,96]{0,1:T(8,128)} %param.23) | copy-start | bytes 884740
  195.6 14.8 %copy-start.35 = (f32[2,768,96]{1,2,0:T(8,128)S(1)}, f32[2,768,96]{1,2,0:T(8,128)}, u32[]{:S(2)}) copy-start(f32[2,768,96]{1,2,0:T(8,128)} %param.30) | copy-start | bytes 1769476
  207.7 4.6 %copy-start.45 = (f32[6,96]{1,0:T(8,128)}, f32[6,96]{1,0:T(8,128)S(1)}, u32[]{:S(2)}) copy-start(f32[6,96]{1,0:T(8,128)S(1)} %get-tuple-element.245) | copy-start | bytes 6916
  218.9 4.4 %copy-start.40 = (f32[12,8]{0,1:T(8,128)}, f32[12,8]{0,1:T(8,128)S(1)}, u32[]{:S(2)}) copy-start(f32[12,8]{0,1:T(8,128)S(1)} %copy.307) | copy-start | bytes 1156
  226.5 3.5 %copy-start.16 = (bf16[394,768]{1,0:T(8,128)(2,1)S(1)}, bf16[394,768]{1,0:T(8,128)(2,1)}, u32[]{:S(2)}) copy-start(bf16[394,768]{1,0:T(8,128)(2,1)} %get-tuple-element.161) | copy-start | bytes 1815556
  (31 other events, 39.9 us)
where the time goes:
time: 234 us; the launch traced here: 233 us
  Pallas kernels  136 us (58%)
  local copies, waits for them, and re-layouts  45 us (19%)
  matrix products  27.4 us (12%)
  other arithmetic  23 us (10%)
    pallas_call x5, Pallas kernels, exchange(): pl.pallas_call(kernel, out_shape=tuple(outs), in_specs=[pl.BlockSpec(memo...  136 us
    unnamed x136, local copies, waits for them, and re-layouts  22.9 us
    dot_general x1, matrix products, on_device(): jnp.dot(normed_two, widen, preferred_element_type=jnp.float32) + hidden_bias  5.56 us
    another operation x12, other arithmetic, adamw(): return (fresh, jnp.stack([first, second]))  5.07 us

commit v1 on v0

--- a/solution.py
+++ b/solution.py
@@ -293,7 +293,7 @@
     return jnp.pad(values, [(0, 0)] * (values.ndim - 1) + [(0, lanes - values.shape[-1])])
 
 
-def on_device(
+def plain_step(
     fsdp,
     tensor,
     block_input,
@@ -508,6 +508,658 @@
         + tuple(owned)
         + tuple((entry[0] for entry in stepped))
         + tuple((entry[1] for entry in stepped))
+    )
+
+
+def fused(fsdp, tensor, dims, args):
+    images, seqlen, width, owned, feat, hidden, c_fc, c_qv, n_qv = dims
+    low, f32 = jnp.bfloat16, jnp.float32
+    far_n, across_n = fsdp // 2, tensor // 2
+    heads = feat // HD
+    padded = args[0].shape[1]
+    rows = images * padded
+    lanes = args[6].shape[1]
+    half = width // 2
+    part = owned // 2
+    wide = 3 * feat + HD
+    combined = 4 * feat
+    share = 1.0 / tensor
+
+    def kernel(
+        x_ref, gy_ref, wq_ref, wo_ref, w1_ref, w2_ref, small_ref,
+        own_g, own_1, own_2, out_ref, in_ref, tot_ref,
+        gg, g1, g2, gs, vec, bias, n1, r1, h1, qs, ks, vs, ps, os, x1, n2, r2, h2, slope, us, gfb,
+        gx, gxb, gqkv, t_in, t_core, t_half, t_across, t_out,
+        rs_in, rs_near, rs_sum, rs_far, sm,
+        bsem_s, bsem_r, ysem_s, ysem_r, tsem_s, tsem_r, rsem_s, rsem_r, ssem_s, ssem_r,
+    ):
+        mine = lax.axis_index("fsdp")
+        lane = lax.axis_index("tensor")
+        far, near = lax.div(mine, 2), lax.rem(mine, 2)
+        across, core = lax.div(lane, 2), lax.rem(lane, 2)
+        twin = (2 * far + (1 - near), lane)
+        mate = (mine, 2 * across + (1 - core))
+
+        def ahead(step):
+            return lax.rem(far + step, far_n)
+
+        def behind(step):
+            return lax.rem(far + far_n - step, far_n)
+
+        def other_x(step):
+            return (mine, 2 * lax.rem(across + step, across_n) + core)
+
+        barrier = pltpu.get_barrier_semaphore()
+        peers = [twin, mate]
+        peers += [(2 * ahead(j) + near, lane) for j in range(1, far_n)]
+        peers += [other_x(j) for j in range(1, across_n)]
+        for who in peers:
+            pl.semaphore_signal(barrier, inc=1, device_id=who, device_id_type=MESH_ID)
+
+        def copy(src, dst, send, recv, target):
+            return pltpu.make_async_remote_copy(
+                src_ref=src, dst_ref=dst, send_sem=send, recv_sem=recv,
+                device_id=target, device_id_type=MESH_ID,
+            )
+
+        pending = []
+
+        def begin(entry):
+            entry.start()
+            pending.append(entry)
+
+        gs[mine] = small_ref[...]
+        out_t = wo_ref[...].T.astype(low)
+        gg[mine] = jnp.concatenate(
+            [wq_ref[0].astype(low), wq_ref[1].astype(low), wq_ref[2].astype(low), out_t], axis=1
+        )
+        g1[mine] = w1_ref[...].astype(low)
+        g2[mine] = w2_ref[...].astype(low)
+        pl.semaphore_wait(barrier, len(peers))
+
+        units = [(gs, None)]
+        for ref in (gg, g1, g2):
+            units += [(ref, 0), (ref, 1)]
+
+        def place(u, slot):
+            ref, piece = units[u]
+            if piece is None:
+                return ref.at[slot]
+            return ref.at[slot, pl.ds(piece * part, part)]
+
+        def ring(u, s):
+            slot = place(u, 2 * behind(s - 1) + near)
+            return copy(slot, slot, bsem_s.at[u, s], bsem_r.at[u, s], (2 * ahead(1) + near, lane))
+
+        def ring_wait(u, s):
+            slot = place(u, 2 * behind(s) + near)
+            copy(slot, slot, bsem_s.at[u, s], bsem_r.at[u, s], (2 * ahead(1) + near, lane)).wait_recv()
+
+        def cross(u, s):
+            slot = place(u, 2 * behind(s) + near)
+            return copy(slot, slot, ysem_s.at[u, s], ysem_r.at[u, s], twin)
+
+        def cross_wait(u):
+            for s in range(far_n):
+                slot = place(u, 2 * behind(s) + (1 - near))
+                copy(slot, slot, ysem_s.at[u, s], ysem_r.at[u, s], twin).wait_recv()
+
+        groups = [(0, 1, 2), (3, 4), (5, 6)]
+
+        def gather():
+            for u in groups[0]:
+                begin(ring(u, 1))
+                begin(cross(u, 0))
+            for index, group in enumerate(groups):
+                after = groups[index + 1] if index + 1 < len(groups) else ()
+                for s in range(1, far_n):
+                    for u in group:
+                        yield
+                        ring_wait(u, s)
+                        if s + 1 < far_n:
+                            begin(ring(u, s + 1))
+                        begin(cross(u, s))
+                    if s + 2 >= far_n and s + 1 < far_n or far_n == 2:
+                        for u in after:
+                            begin(ring(u, 1))
+                for u in after:
+                    begin(cross(u, 0))
+
+        flow = gather()
+
+        def step(count=1):
+            for _ in range(count):
+                next(flow, None)
+
+        step(1)
+
+        for i in range(images):
+            xf = x_ref[i].astype(f32)
+            center = xf - jnp.mean(xf, axis=-1, keepdims=True)
+            scale = lax.rsqrt(jnp.mean(center * center, axis=-1, keepdims=True) + epsilon)
+            n1[i] = center * scale
+            r1[i] = scale
+        per_group = 3 * (far_n - 1)
+        step(per_group)
+        cross_wait(0)
+
+        def spread(d, carry):
+            rows_d = gs[d]
+            source = lax.broadcasted_iota(jnp.int32, (lanes, width), 0)
+            target = lax.broadcasted_iota(jnp.int32, (lanes, width), 1)
+            pick = ((target == d * owned + source) & (source < owned)).astype(f32).astype(low)
+            first = jnp.dot(rows_d, pick, preferred_element_type=f32)
+            source = lax.broadcasted_iota(jnp.int32, (lanes, hidden), 0)
+            target = lax.broadcasted_iota(jnp.int32, (lanes, hidden), 1)
+            at = lax.div(source, c_fc) * (c_fc * fsdp) + d * c_fc + lax.rem(source, c_fc)
+            pick = ((target == at) & (source * fsdp < hidden)).astype(f32).astype(low)
+            second = jnp.dot(rows_d, pick, preferred_element_type=f32)
+            source = lax.broadcasted_iota(jnp.int32, (lanes, wide), 0)
+            target = lax.broadcasted_iota(jnp.int32, (lanes, wide), 1)
+            at = lax.div(source, c_qv) * (c_qv * fsdp) + d * c_qv + lax.rem(source, c_qv)
+            at = jnp.where(at < feat, at, at + feat)
+            pick = ((target == at) & (source < n_qv)).astype(f32).astype(low)
+            third = jnp.dot(rows_d, pick, preferred_element_type=f32)
+            return (carry[0] + first, carry[1] + second, carry[2] + third)
+
+        small_rows = small_ref.shape[0]
+        start = tuple(jnp.zeros((small_rows, w), f32) for w in (width, hidden, wide))
+        spread_v, spread_h, spread_q = lax.fori_loop(0, fsdp, spread, start)
+        vec[...] = spread_v
+        gain1, shift1, gain2, shift2, bias_o, bias_2 = (vec[r : r + 1] for r in range(6))
+        bias_f = spread_h[6:7]
+        bias[...] = spread_q[7:8]
+        for i in range(images):
+            h1[i] = (n1[i] * gain1 + shift1).astype(low)
+        cross_wait(1)
+        cross_wait(2)
+
+        def flat(ref):
+            return ref[...].reshape(ref.shape[0] * ref.shape[1], ref.shape[2])
+
+        def cols(ref, start, size):
+            piece = ref[:, :, start : start + size]
+            return piece.reshape(ref.shape[0] * ref.shape[1], size)
+
+        span = feat + HD
+        k_at, v_at, o_at = feat - HD, 2 * feat, combined - span
+        head_of = lax.broadcasted_iota(jnp.int32, (padded, span), 1) // HD
+        key_at = lax.broadcasted_iota(jnp.int32, (padded, padded), 1)
+
+        def nn(a, b):
+            return jnp.dot(a, b, preferred_element_type=f32)
+
+        def nt(a, b):
+            return lax.dot_general(a, b, (((1,), (1,)), ((), ())), preferred_element_type=f32)
+
+        def tn(a, b):
+            return lax.dot_general(a, b, (((0,), (0,)), ((), ())), preferred_element_type=f32)
+
+        mine_half = pl.ds(pl.multiple_of(core * half, half), half)
+        mate_half = pl.ds(pl.multiple_of((1 - core) * half, half), half)
+
+        def total(k, i):
+            def sem(ref, index):
+                return ref.at[k, i, index]
+
+            first = copy(t_in.at[k, i, :, mate_half], t_core.at[k, i], sem(tsem_s, 0),
+                         sem(tsem_r, 0), mate)
+            begin(first)
+            yield
+            first.wait_recv()
+            mine_sum = t_in[k, i, :, mine_half].astype(f32) + t_core[k, i].astype(f32)
+            t_half[k, i] = mine_sum.astype(low)
+            hops = []
+            for j in range(1, across_n):
+                hops.append(copy(t_half.at[k, i], t_across.at[k, i, j - 1], sem(tsem_s, 1 + j),
+                                 sem(tsem_r, 1 + j), other_x(j)))
+                begin(hops[-1])
+            yield
+            summed = t_half[k, i].astype(f32)
+            for j in range(1, across_n):
+                hops[j - 1].wait_recv()
+                summed = summed + t_across[k, i, j - 1].astype(f32)
+            t_out[k, i, :, mine_half] = summed.astype(low)
+            own = t_out.at[k, i, :, mine_half]
+            begin(copy(own, own, sem(tsem_s, 1), sem(tsem_r, 1), mate))
+            yield
+            theirs = t_out.at[k, i, :, mate_half]
+            copy(theirs, theirs, sem(tsem_s, 1), sem(tsem_r, 1), mate).wait_recv()
+            yield
+
+        sums = {}
+
+        def project(i):
+            pr = nn(h1[i], cols(gg, 0, wide)) + bias[...]
+            qs[i] = pltpu.roll(pr[:, :span], HD, 1).astype(low)
+            ks[i] = pr[:, k_at : k_at + span].astype(low)
+            vs[i] = pr[:, v_at : v_at + span].astype(low)
+
+        def attend_head(i, h, mixed):
+            q_h = jnp.where(head_of == h + 1, qs[i], jnp.zeros_like(qs[i]))
+            s = nt(q_h, ks[i]) * 0.125
+            s = jnp.where(key_at < seqlen, s, -1e30)
+            e = jnp.exp(s - jnp.max(s, axis=-1, keepdims=True))
+            p = e * (1.0 / jnp.sum(e, axis=-1, keepdims=True))
+            ps[i, h] = p
+            o_h = nn(p.astype(low), vs[i])
+            return jnp.where(head_of == h, o_h, mixed)
+
+        attn = []
+        for i in range(images):
+            project(i)
+            step(1)
+            mixed = jnp.zeros((padded, span), f32)
+            for h in range(heads):
+                mixed = attend_head(i, h, mixed)
+                step(1)
+                for entry in attn:
+                    if h < 2:
+                        next(entry)
+            os[i] = pltpu.roll(mixed, HD, 1).astype(low)
+            t_in[0, i] = nt(os[i], cols(gg, o_at, span)).astype(low)
+            attn.append(total(0, i))
+            next(attn[i])
+            step(1)
+        step(2)
+        next(attn[0], None) if images > 1 and heads < 2 else None
+        next(attn[-1])
+        gy_sum = None
+        for i in range(images):
+            add = jnp.sum(gy_ref[i].astype(f32), axis=0, keepdims=True)
+            gy_sum = add if gy_sum is None else gy_sum + add
+        step(1)
+        for entry in attn:
+            for _ in entry:
+                pass
+        step(100)
+
+        for i in range(images):
+            res = x_ref[i].astype(f32) + t_out[0, i].astype(f32) + bias_o
+            x1[i] = res
+            center = res - jnp.mean(res, axis=-1, keepdims=True)
+            scale = lax.rsqrt(jnp.mean(center * center, axis=-1, keepdims=True) + epsilon)
+            unit = center * scale
+            n2[i] = unit
+            r2[i] = scale
+            h2[i] = (unit * gain2 + shift2).astype(low)
+        cross_wait(3)
+        cross_wait(4)
+        for i in range(images):
+            f = nn(h2[i], flat(g1)) + bias_f
+            phi = 0.5 * (1.0 + lax.erf(f * sqrt_half))
+            us[i] = (f * phi).astype(low)
+            slope[i] = phi + f * jnp.exp(-0.5 * f * f) * inv_root
+        cross_wait(5)
+        cross_wait(6)
+        two, mlp = [], []
+        gf_sum = None
+        row2 = row3 = None
+
+        def plus(a, b):
+            return b if a is None else a + b
+
+        for i in range(images):
+            gf = nn(gy_ref[i], flat(g2)) * slope[i]
+            gfb[i] = gf.astype(low)
+            gf_sum = plus(gf_sum, jnp.sum(gf, axis=0, keepdims=True))
+            t_in[1, i] = nt(gfb[i], flat(g1)).astype(low)
+            two.append(total(1, i))
+            next(two[i])
+
+        def scatter_y(p):
+            for j in list(range(1, far_n)) + [0]:
+                begin(copy(rs_in.at[p, 2 * ahead(j) + (1 - near)], rs_near.at[p, j],
+                           rsem_s.at[p, j], rsem_r.at[p, j], twin))
+
+        def scatter_z(p, j):
+            block = rs_in.at[p, 2 * ahead(j) + (1 - near)]
+            copy(block, rs_near.at[p, j], rsem_s.at[p, j], rsem_r.at[p, j], twin).wait_recv()
+            rs_sum[p, j - 1] = (
+                rs_in[p, 2 * ahead(j) + near].astype(f32) + rs_near[p, j].astype(f32)
+            ).astype(low)
+            begin(copy(rs_sum.at[p, j - 1], rs_far.at[p, j - 1], rsem_s.at[p, far_n + j],
+                       rsem_r.at[p, far_n + j], (2 * ahead(j) + near, lane)))
+
+        def scatter_end(p, ref):
+            block = rs_in.at[p, 2 * far + (1 - near)]
+            copy(block, rs_near.at[p, 0], rsem_s.at[p, 0], rsem_r.at[p, 0], twin).wait_recv()
+            acc = rs_in[p, mine].astype(f32) + rs_near[p, 0].astype(f32)
+            for j in range(1, far_n):
+                copy(rs_sum.at[p, j - 1], rs_far.at[p, j - 1], rsem_s.at[p, far_n + j],
+                     rsem_r.at[p, far_n + j], (2 * ahead(j) + near, lane)).wait_recv()
+                acc = acc + rs_far[p, j - 1].astype(f32)
+            ref[...] = acc
+
+        def blocks(grad):
+            return grad.astype(low).reshape(fsdp, owned, grad.shape[1])
+
+        for i in range(images):
+            next(two[i])
+        rs_in[0] = blocks(tn(flat(gy_ref), flat(us)))
+        rs_in[1] = blocks(tn(flat(h2), flat(gfb)))
+        scatter_y(0)
+        scatter_y(1)
+        for i in range(images):
+            t_in[2, i] = nt(us[i], flat(g2)).astype(low)
+        for i in range(images):
+            term = t_in[1, i].astype(f32)
+            row2 = plus(row2, jnp.sum(term * n2[i], axis=0, keepdims=True))
+            row3 = plus(row3, jnp.sum(term, axis=0, keepdims=True))
+        for i in range(images):
+            next(two[i])
+        for i in range(images):
+            mlp.append(total(2, i))
+            next(mlp[i])
+        for i in range(images):
+            next(two[i])
+            next(mlp[i])
+
+        events = [(p, j) for p in range(2) for j in range(1, far_n)]
+
+        def reduce_step():
+            if events:
+                scatter_z(*events.pop(0))
+
+        gx_sum = row7 = row0 = row1 = None
+        one = []
+        for i in range(images):
+            e = t_out[1, i].astype(f32) * gain2
+            unit = n2[i]
+            g = gy_ref[i].astype(f32) + r2[i] * (
+                e
+                - jnp.mean(e, axis=-1, keepdims=True)
+                - unit * jnp.mean(e * unit, axis=-1, keepdims=True)
+            )
+            gx[i] = g
+            gxb[i] = g.astype(low)
+            gx_sum = plus(gx_sum, jnp.sum(g, axis=0, keepdims=True))
+            go = nn(gxb[i], cols(gg, o_at, span))
+            go = pltpu.roll(go, span - HD, 1).astype(low)
+            dq = jnp.zeros((padded, span), f32)
+            dk = jnp.zeros((padded, span), f32)
+            dv = jnp.zeros((padded, span), f32)
+            for h in range(heads):
+                go_h = jnp.where(head_of == h, go, jnp.zeros_like(go))
+                p = ps[i, h]
+                gp = nt(go_h, vs[i])
+                gs_h = (p * (gp - jnp.sum(p * gp, axis=-1, keepdims=True))).astype(low)
+                dq = jnp.where(head_of == h + 1, nn(gs_h, ks[i]), dq)
+                dk = jnp.where(head_of == h + 1, tn(gs_h, qs[i]), dk)
+                dv = jnp.where(head_of == h, tn(p.astype(low), go), dv)
+                reduce_step()
+            dq = pltpu.roll(dq, span - HD, 1) * 0.125
+            dk = dk * 0.125
+            edge = 2 * HD
+            pieces = jnp.concatenate(
+                [dq[:, :edge], dq[:, edge:] + dk[:, :edge], dk[:, edge:], dv], axis=1
+            )
+            gqkv[i] = pieces.astype(low)
+            row7 = plus(row7, jnp.sum(pieces, axis=0, keepdims=True))
+            term = nt(gqkv[i], cols(gg, 0, wide)).astype(low)
+            t_in[3, i] = term
+            one.append(total(3, i))
+            next(one[i])
+            term = term.astype(f32)
+            row0 = plus(row0, jnp.sum(term * n1[i], axis=0, keepdims=True))
+            row1 = plus(row1, jnp.sum(term, axis=0, keepdims=True))
+
+        grad = tn(flat(h1), flat(gqkv))
+        outer = tn(flat(gxb), flat(os))
+        rs_in[2, :, :, :o_at] = blocks(grad[:, :o_at])
+        tail = grad[:, o_at:]
+        rs_in[2, :, :, o_at : o_at + tail.shape[1]] = blocks(
+            tail + outer[:, : tail.shape[1]]
+        )
+        rs_in[2, :, :, o_at + tail.shape[1] :] = blocks(outer[:, tail.shape[1] :])
+
+        mine_rows = sm.at[0]
+        sm[0, 0:1] = row0
+        sm[0, 1:2] = row1
+        sm[0, 2:3] = row2
+        sm[0, 3:4] = row3
+        sm[0, 4:5] = gx_sum * share
+        sm[0, 5:6] = gy_sum * share
+        sm[0, 6:7] = gf_sum
+        sm[0, 7:8] = jnp.zeros((1, width), f32)
+        sm[0, 7:8, :wide] = row7
+        while events:
+            reduce_step()
+        for i in range(images):
+            next(one[i])
+        scatter_y(2)
+        shared = lax.broadcasted_iota(jnp.int32, (8, width), 0) < 6
+
+        def small_flow():
+            hop = copy(sm.at[0], sm.at[1], ssem_s.at[0], ssem_r.at[0], mate)
+            begin(hop)
+            yield
+            hop.wait_recv()
+            sm[2] = sm[0] + jnp.where(shared, sm[1], 0.0)
+            hops = []
+            for j in range(1, across_n):
+                hops.append(copy(sm.at[2], sm.at[2 + j], ssem_s.at[j], ssem_r.at[j], other_x(j)))
+                begin(hops[-1])
+            yield
+            summed = sm[2]
+            for j in range(1, across_n):
+                hops[j - 1].wait_recv()
+                summed = summed + jnp.where(shared, sm[2 + j], 0.0)
+            base = 2 + across_n
+            sm[base] = summed
+            hop = copy(sm.at[base], sm.at[base + 1], ssem_s.at[across_n], ssem_r.at[across_n], twin)
+            begin(hop)
+            yield
+            hop.wait_recv()
+            sm[base + 2] = sm[base] + sm[base + 1]
+            hops = []
+            for j in range(1, far_n):
+                hops.append(copy(sm.at[base + 2], sm.at[base + 2 + j], ssem_s.at[across_n + j],
+                                 ssem_r.at[across_n + j], (2 * ahead(j) + near, lane)))
+                begin(hops[-1])
+            yield
+            summed = sm[base + 2]
+            for j in range(1, far_n):
+                hops[j - 1].wait_recv()
+                summed = summed + sm[base + 2 + j]
+            tot_ref[...] = summed
+            yield
+
+        tiny = small_flow()
+        next(tiny)
+        for entry in mlp:
+            next(entry)
+        next(tiny)
+        for i in range(images):
+            next(one[i])
+        next(tiny)
+        scatter_end(0, own_2)
+        next(tiny)
+        scatter_end(1, own_1)
+        for entry in mlp:
+            for _ in entry:
+                pass
+        for i in range(images):
+            out_ref[i] = (x1[i] + t_out[2, i].astype(f32) + bias_2).astype(low)
+        for j in range(1, far_n):
+            scatter_z(2, j)
+        next(tiny)
+        for i in range(images):
+            for _ in one[i]:
+                pass
+            e = t_out[3, i].astype(f32) * gain1
+            unit = n1[i]
+            in_ref[i] = gx[i] + r1[i] * (
+                e
+                - jnp.mean(e, axis=-1, keepdims=True)
+                - unit * jnp.mean(e * unit, axis=-1, keepdims=True)
+            )
+        scatter_end(2, own_g)
+        for entry in pending:
+            entry.wait_send()
+
+    shape = jax.ShapeDtypeStruct
+    outs = (
+        shape((owned, combined), f32),
+        shape((owned, hidden), f32),
+        shape((owned, hidden), f32),
+        shape((images, padded, width), low),
+        shape((images, padded, width), f32),
+        shape((8, width), f32),
+    )
+    span = feat + HD
+    sp = (images, padded)
+
+    def vm(dims, kind):
+        return pltpu.VMEM(dims, kind)
+
+    few = max(far_n - 1, 1)
+    xs = max(across_n - 1, 1)
+    dma = pltpu.SemaphoreType.DMA
+    scratch = [
+        vm((fsdp, owned, combined), low),
+        vm((fsdp, owned, hidden), low),
+        vm((fsdp, owned, hidden), low),
+        vm((fsdp,) + args[6].shape, low),
+        vm((args[6].shape[0], width), f32),
+        vm((1, wide), f32),
+        vm(sp + (width,), f32), vm(sp + (1,), f32), vm(sp + (width,), low),
+        vm(sp + (span,), low), vm(sp + (span,), low), vm(sp + (span,), low),
+        vm((images, heads, padded, padded), f32),
+        vm(sp + (span,), low),
+        vm(sp + (width,), f32),
+        vm(sp + (width,), f32), vm(sp + (1,), f32), vm(sp + (width,), low),
+        vm(sp + (hidden,), f32), vm(sp + (hidden,), low), vm(sp + (hidden,), low),
+        vm(sp + (width,), f32), vm(sp + (width,), low), vm(sp + (wide,), low),
+        vm((4,) + sp + (width,), low),
+        vm((4,) + sp + (half,), low), vm((4,) + sp + (half,), low),
+        vm((4, images, xs, padded, half), low),
+        vm((4,) + sp + (width,), low),
+        vm((3, fsdp, owned, combined), low),
+        vm((3, far_n, owned, combined), low),
+        vm((3, few, owned, combined), low),
+        vm((3, few, owned, combined), low),
+        vm((4 + across_n + far_n, 8, width), f32),
+        dma((7, far_n)), dma((7, far_n)), dma((7, far_n)), dma((7, far_n)),
+        dma((4, images, 1 + across_n)), dma((4, images, 1 + across_n)),
+        dma((3, 2 * far_n)), dma((3, 2 * far_n)),
+        dma((across_n + far_n,)), dma((across_n + far_n,)),
+    ]
+    space = pl.BlockSpec(memory_space=pltpu.VMEM)
+    return pl.pallas_call(
+        kernel,
+        out_shape=outs,
+        in_specs=[space] * len(args),
+        out_specs=tuple([space] * len(outs)),
+        scratch_shapes=scratch,
+        compiler_params=pltpu.CompilerParams(
+            collective_id=1, has_side_effects=True, vmem_limit_bytes=60 * 1024 * 1024
+        ),
+        name="fused_layer",
+    )(*args)
+
+
+def update(own, params, moments):
+    count = len(own)
+
+    def kernel(*refs):
+        g_in, p_in, m_in = refs[:count], refs[count : 2 * count], refs[2 * count : 3 * count]
+        p_out, m_out = refs[3 * count : 4 * count], refs[4 * count : 5 * count]
+        for g, p, m, np_, nm in zip(g_in, p_in, m_in, p_out, m_out):
+            grad, param = g[...], p[...]
+            first = 0.9 * m[0] + 0.1 * grad
+            second = 0.999 * m[1] + 0.001 * grad * grad
+            np_[...] = param - 0.004 * (
+                first / corr_one / (jnp.sqrt(second / corr_two) + 1e-08) + 0.05 * param
+            )
+            nm[0] = first
+            nm[1] = second
+
+    shape = jax.ShapeDtypeStruct
+    outs = [shape(p.shape, jnp.float32) for p in params]
+    outs += [shape(m.shape, jnp.float32) for m in moments]
+    space = pl.BlockSpec(memory_space=pltpu.VMEM)
+    result = pl.pallas_call(
+        kernel,
+        out_shape=tuple(outs),
+        in_specs=[space] * (3 * count),
+        out_specs=tuple([space] * len(outs)),
+        compiler_params=pltpu.CompilerParams(vmem_limit_bytes=40 * 1024 * 1024),
+        name="update",
+    )(*own, *params, *moments)
+    return result[:count], result[count:]
+
+
+def on_device(fsdp, tensor, *args):
+    owned = args[3].shape[0]
+    local = args[3].shape[2]
+    fits = (
+        owned % 16 == 0
+        and (local + HD) % 128 == 0
+        and 4 * local == args[0].shape[2] == args[5].shape[1]
+        and fsdp % 2 == 0
+        and fsdp <= 16
+    )
+    return (fused_step if fits else plain_step)(fsdp, tensor, *args)
+
+
+def fused_step(
+    fsdp, tensor, block_input, output_grad, live_images, w_qkv, w_out, w_fc1, w_fc2, qv_bias,
+    fc1_bias, norm_vec, mom_qkv, mom_out, mom_fc1, mom_fc2, mom_qvb, mom_fc1b, mom_vec,
+):
+    low, f32 = jnp.bfloat16, jnp.float32
+    images, seqlen, width = block_input.shape
+    owned, _, feat = w_qkv.shape
+    hidden = w_fc1.shape[1]
+    n_qv, n_fc = qv_bias.size, fc1_bias.size
+    vec_rows = norm_vec.shape[0]
+    lanes = -(-max(owned, n_qv, n_fc) // 128) * 128
+    padded = -(-seqlen // 16) * 16
+    live = live_images.astype(low)[:, None, None]
+    edge = ((0, 0), (0, padded - seqlen), (0, 0))
+    x_pad = jnp.pad(block_input, edge)
+    gy_pad = jnp.pad(output_grad * live, edge)
+    small = jnp.concatenate(
+        [
+            row_of(norm_vec, lanes),
+            row_of(fc1_bias.reshape(1, n_fc), lanes),
+            row_of(qv_bias.reshape(1, n_qv), lanes),
+            jnp.zeros((16 - vec_rows - 2, lanes), f32),
+        ]
+    ).astype(low)
+    dims = (images, seqlen, width, owned, feat, hidden, fc1_bias.shape[1], qv_bias.shape[2], n_qv)
+    wq, w2 = w_qkv.transpose(1, 0, 2), w_fc2.T
+    own_g, own_1, own_2, out_rows, in_rows, sums = fused(
+        fsdp, tensor, dims, (x_pad, gy_pad, wq, w_out, w_fc1, w2, small)
+    )
+    block_output = out_rows[:, :seqlen] * live
+    input_grad = in_rows[:, :seqlen]
+    g_qkv = jnp.stack([own_g[:, c * feat : (c + 1) * feat] for c in range(3)])
+    g_out = own_g[:, 3 * feat :].T
+    news, moms = update(
+        (g_qkv, g_out, own_1, own_2),
+        (wq, w_out, w_fc1, w2),
+        (mom_qkv.transpose(0, 2, 1, 3), mom_out, mom_fc1, mom_fc2.transpose(0, 2, 1)),
+    )
+    mine = lax.axis_index("fsdp")
+    g_vec = lax.dynamic_slice(sums, (0, mine * owned), (vec_rows, owned))
+    r_fc, c_fc = fc1_bias.shape
+    g_fc1b = lax.dynamic_slice(
+        sums[vec_rows].reshape(r_fc, fsdp * c_fc), (0, mine * c_fc), (r_fc, c_fc)
+    )
+    k_qv, r_qv, c_qv = qv_bias.shape
+    row = sums[vec_rows + 1]
+    pair = jnp.stack([row[:feat], row[2 * feat : 3 * feat]]).reshape(k_qv, r_qv, fsdp * c_qv)
+    g_qvb = lax.dynamic_slice(pair, (0, 0, mine * c_qv), (k_qv, r_qv, c_qv))
+    qvb = adamw(qv_bias, g_qvb, mom_qvb)
+    fcb = adamw(fc1_bias, g_fc1b, mom_fc1b)
+    nvec = adamw(norm_vec, g_vec, mom_vec)
+    return (
+        block_output, input_grad,
+        g_qkv.transpose(1, 0, 2), g_out, own_1, own_2.T, g_qvb, g_fc1b, g_vec,
+        news[0].transpose(1, 0, 2), news[1], news[2], news[3].T, qvb[0], fcb[0], nvec[0],
+        moms[0].transpose(0, 2, 1, 3), moms[1], moms[2], moms[3].transpose(0, 2, 1),
+        qvb[1], fcb[1], nvec[1],
     )
 
 

time: 234 us -> 149 us (0.64)
  matrix products: 27.4 us -> 0 us
  local copies, waits for them, and re-layouts: 45 us -> 21 us
  Pallas kernels: 136 us -> 118 us
  other arithmetic: 23 us -> 8.14 us
    dot_general x18 -> x0, matrix products: 27.4 us -> none  [the longest x1 5.56 us: on_device(): jnp.dot(normed_two, widen, preferred_element_type=jnp.float32) + hidden_bias]
    pallas_call x5 -> x2, Pallas kernels: 136 us -> 118 us  [the longest x1 116 us: fused(): pl.pallas_call(kernel, out_shape=outs, in_specs=[space] * len(args), out_...]
    unnamed x136 -> x61, local copies, waits for them, and re-layouts: 22.9 us -> 10.2 us
    reduce_sum x9 -> x0, other arithmetic: 9.69 us -> none  [the longest x1 3.58 us: on_device(): jnp.sum(delta_resid, axis=0)]
    convert_element_type x11 -> x0, local copies, waits for them, and re-layouts: 7.79 us -> none  [the longest x2 1.96 us: blocks(): return grad.astype(low).reshape(fsdp, owned_rows, grad.shape[1])]
    reshape x13 -> x2, local copies, waits for them, and re-layouts: 7 us -> 0.19 us  [the longest x1 0.1 us: fused_step(): fc1_bias.reshape(1, n_fc)]
    convert_element_type x6 -> x1, other arithmetic: 3.72 us -> 0.01 us  [fused_step(): live = live_images.astype(low)[:, None, None]]
    add x5 -> x0, other arithmetic: 3.25 us -> none  [the longest x1 3.13 us: on_device(): delta_resid + norm_backward(delta_one, unit_one, scale_one, vecf[0])]
where the time goes in v1:
time: 149 us; the launch traced here: 148 us
  Pallas kernels  118 us (79%)
  local copies, waits for them, and re-layouts  21 us (14%)
  other arithmetic  8.14 us (5%)
    pallas_call x1, Pallas kernels, fused(): pl.pallas_call(kernel, out_shape=outs, in_specs=[space] * len(args), out_...  116 us
    unnamed x61, local copies, waits for them, and re-layouts  10.2 us
    another operation x6, other arithmetic, adamw(): return (fresh, jnp.stack([first, second]))  3.21 us

profile of v1, /device:TPU:0, one launch (start us, length us, event | category | flops | bytes accessed | tf_op | source)
XLA Modules:
  0.0 148.3 jit_solution(1597660063467818172)
XLA Ops:
  0.7 1.2 copy.53
  1.9 0.9 pad.22.x_ref
  2.9 0.9 pad.23.gy_ref
  4.9 116.5 %fused_layer.1 = (f32[96,768]{1,0:T(8,128)}, f32[96,768]{1,0:T(8,128)}, f32[96,768]{1,0:T(8,128)}, bf16[2,208,768]{2,1,0:T(8,128)(2,1)}, f32[2,208,768]{2,1,0:T(8,128)}, /*index=5*/f32[8,768]{1,0:T(8,128)}) custom-call(bf16[2,208,768]{2,1,0:T(8,128)(2,1)} %pad.22.x_ref, bf16[2,208,768]{2,1,0:T(8,128)(2,1)} %pad.23.gy_ref, f32[3,96,192]{2,1,0:T(8,128)} %bitcast.63, ...), custom_call_target="tpu_custom_call" | custom-call | tf_op jit(solution)/shard_map/fused_layer/pallas_call | solution.py:1049
  121.4 1.3 slice_multiply_fusion
  122.7 1.3 copy.67
  124.1 1.6 %copy.68 = f32[2,197,768]{2,0,1:T(2,128)} copy(f32[2,197,768]{2,1,0:T(8,128)S(1)} %slice.51) | data formatting | bytes 2420736
  125.9 0.8 pad_maximum_fusion
  126.7 1.9 %copy.57 = f32[96,768]{0,1:T(8,128)} copy(f32[96,768]{1,0:T(8,128)} %get-tuple-element.39) | data formatting | bytes 589824 | tf_op jit(solution)/shard_map/fused_layer/pallas_call | solution.py:1049
  128.5 1.5 %slice_bitcast_fusion.refs_1_ = f32[192,96]{1,0:T(8,128)} fusion(f32[96,768]{0,1:T(8,128)} %copy.57), kind=kLoop, calls=%fused_computation.3 | loop fusion | bytes 147456 | tf_op jit(solution)/shard_map/transpose | solution.py:1138
  130.1 0.7 multiply_bitcast_fusion
  130.8 1.3 slice_reduce_fusion.2
  132.1 0.8 stack.53
  132.8 1.3 stack.52
  134.2 1.4 copy_subtract_fusion
  136.1 0.8 slice_reduce_fusion
  137.1 0.8 fusion.22
  137.9 0.8 fusion.16
  138.7 0.9 copy-done.8
  139.6 0.9 copy-done.9
  140.5 0.9 copy-done.10
  141.5 1.8 %update.1 = (f32[3,96,192]{2,1,0:T(8,128)}, f32[192,96]{1,0:T(8,128)}, f32[96,768]{1,0:T(8,128)}, f32[96,768]{1,0:T(8,128)}, f32[2,3,96,192]{3,2,1,0:T(8,128)}, ...) custom-call(f32[3,96,192]{2,1,0:T(8,128)S(1)} %get-tuple-element.105.refs_0_, ...), custom_call_target="tpu_custom_call" | custom-call | tf_op jit(solution)/shard_map/update/pallas_call | solution.py:1082
  146.9 0.7 copy.110
  147.6 0.7 copy.111
  (75 shorter events, 5.9 us)
Async XLA Ops:
  0.7 2.1 %copy-start.13 = (bf16[2,197,768]{2,0,1:T(2,128)(2,1)S(1)}, bf16[2,197,768]{2,0,1:T(2,128)(2,1)}, u32[]{:S(2)}) copy-start(bf16[2,197,768]{2,0,1:T(2,128)(2,1)} %param.18) | copy-start | bytes 1815556
  0.7 2.1 %copy-start.25 = (s32[2]{0:T(128)S(1)}, s32[2]{0:T(128)}, u32[]{:S(2)}) copy-start(s32[2]{0:T(128)} %param.19) | copy-start | bytes 28
  2.8 1.0 copy-start.23
  2.8 1.1 copy-start.15
  2.8 1.3 copy-start.17
  121.4 2.6 %copy-start.11 = (f32[2,208,768]{2,1,0:T(8,128)S(1)}, f32[2,208,768]{2,1,0:T(8,128)}, u32[]{:S(2)}) copy-start(f32[2,208,768]{2,1,0:T(8,128)} %get-tuple-element.38) | copy-start | bytes 3833860
  124.1 1.7 %copy-start.12 = (f32[96,768]{1,0:T(8,128)S(1)}, f32[96,768]{1,0:T(8,128)}, u32[]{:S(2)}) copy-start(f32[96,768]{1,0:T(8,128)} %get-tuple-element.39) | copy-start | bytes 884740
  124.1 14.6 %copy-start.6 = (f32[2,96,768]{2,1,0:T(8,128)S(1)}, f32[2,96,768]{2,1,0:T(8,128)}, u32[]{:S(2)}) copy-start(f32[2,96,768]{2,1,0:T(8,128)} %refs_10_.1) | copy-start | bytes 1769476
  124.1 14.6 %copy-start.7 = (f32[2,768,96]{1,2,0:T(8,128)S(1)}, f32[2,768,96]{1,2,0:T(8,128)}, u32[]{:S(2)}) copy-start(f32[2,768,96]{1,2,0:T(8,128)} %param.30) | copy-start | bytes 1769476
  125.8 12.9 %copy-start = (f32[96,3,192]{2,0,1:T(8,128)S(1)}, f32[96,3,192]{2,0,1:T(8,128)}, u32[]{:S(2)}) copy-start(f32[96,3,192]{2,0,1:T(8,128)} %param.20) | copy-start | bytes 663556
  125.8 12.9 %copy-start.1 = (f32[96,768]{1,0:T(8,128)S(1)}, f32[96,768]{1,0:T(8,128)}, u32[]{:S(2)}) copy-start(f32[96,768]{1,0:T(8,128)} %refs_6_.1) | copy-start | bytes 884740
  125.8 12.9 %copy-start.2 = (f32[768,96]{0,1:T(8,128)S(1)}, f32[768,96]{0,1:T(8,128)}, u32[]{:S(2)}) copy-start(f32[768,96]{0,1:T(8,128)} %param.23) | copy-start | bytes 884740
  125.8 12.9 %copy-start.3 = (f32[96,768]{1,0:T(8,128)S(1)}, f32[96,768]{1,0:T(8,128)}, u32[]{:S(2)}) copy-start(f32[96,768]{1,0:T(8,128)} %get-tuple-element.41.refs_3_) | copy-start | bytes 884740
  125.8 12.9 %copy-start.4 = (f32[96,768]{1,0:T(8,128)S(1)}, f32[96,768]{1,0:T(8,128)}, u32[]{:S(2)}) copy-start(f32[96,768]{1,0:T(8,128)} %get-tuple-element.148.refs_2_) | copy-start | bytes 884740
  125.8 12.9 %copy-start.5 = (f32[2,96,3,192]{3,1,2,0:T(8,128)S(1)}, f32[2,96,3,192]{3,1,2,0:T(8,128)}, u32[]{:S(2)}) copy-start(f32[2,96,3,192]{3,1,2,0:T(8,128)} %param.27) | copy-start | bytes 1327108
  137.1 6.8 %copy-start.14 = (f32[12,8]{0,1:T(8,128)}, f32[12,8]{0,1:T(8,128)S(1)}, u32[]{:S(2)}) copy-start(f32[12,8]{0,1:T(8,128)S(1)} %copy.72) | copy-start | bytes 1156
  138.6 5.8 %copy-start.19 = (f32[6,96]{1,0:T(8,128)}, f32[6,96]{1,0:T(8,128)S(1)}, u32[]{:S(2)}) copy-start(f32[6,96]{1,0:T(8,128)S(1)} %get-tuple-element.152) | copy-start | bytes 6916
  140.5 0.9 copy-start.10
  141.4 1.8 %copy-start.22 = (f32[2,3,8]{2,1,0:T(4,128)S(1)}, f32[2,3,8]{2,1,0:T(4,128)}, u32[]{:S(2)}) copy-start(f32[2,3,8]{2,1,0:T(4,128)} %get-tuple-element.101) | copy-start | bytes 580
  141.4 2.4 %copy-start.16 = (f32[12,8]{0,1:T(8,128)S(1)}, f32[12,8]{0,1:T(8,128)}, u32[]{:S(2)}) copy-start(f32[12,8]{0,1:T(8,128)} %param.25) | copy-start | bytes 1156
  141.4 2.4 %copy-start.24 = (f32[2,12,8]{1,2,0:T(8,128)S(1)}, f32[2,12,8]{1,2,0:T(8,128)}, u32[]{:S(2)}) copy-start(f32[2,12,8]{1,2,0:T(8,128)} %param.32) | copy-start | bytes 2308
  141.4 3.0 %copy-start.18 = (f32[6,96]{1,0:T(8,128)S(1)}, f32[6,96]{1,0:T(8,128)}, u32[]{:S(2)}) copy-start(f32[6,96]{1,0:T(8,128)} %param.26) | copy-start | bytes 6916
  141.4 3.7 %copy-start.20 = (f32[2,3,8]{2,1,0:T(4,128)S(1)}, f32[2,3,8]{2,1,0:T(4,128)}, u32[]{:S(2)}) copy-start(f32[2,3,8]{2,1,0:T(4,128)} %get-tuple-element.102) | copy-start | bytes 580
  141.5 3.6 %copy-start.21 = (f32[2,3,8]{2,1,0:T(4,128)S(1)}, f32[2,3,8]{2,1,0:T(4,128)}, u32[]{:S(2)}) copy-start(f32[2,3,8]{2,1,0:T(4,128)} %get-tuple-element.103) | copy-start | bytes 580
  (2 other events, 1.8 us)

commit v2 on v1

--- a/solution.py
+++ b/solution.py
@@ -512,13 +512,17 @@
 
 
 def fused(fsdp, tensor, dims, args):
-    images, seqlen, width, owned, feat, hidden, c_fc, c_qv, n_qv = dims
+    images, seqlen, width, owned, feat, hidden, c_fc, c_qv = dims
     low, f32 = jnp.bfloat16, jnp.float32
     far_n, across_n = fsdp // 2, tensor // 2
     heads = feat // HD
-    padded = args[0].shape[1]
+    padded = -(-seqlen // 16) * 16
     rows = images * padded
-    lanes = args[6].shape[1]
+    vec_rows, r_fc = args[6].shape[0], args[7].shape[1]
+    fc_row = -(-vec_rows // 8) * 8
+    qv_row = fc_row + -(-c_fc // 8) * 8
+    small_rows = -(-(qv_row + 2 * heads) // 16) * 16
+    lanes = -(-max(owned, r_fc, c_qv) // 128) * 128
     half = width // 2
     part = owned // 2
     wide = 3 * feat + HD
@@ -526,9 +530,9 @@
     share = 1.0 / tensor
 
     def kernel(
-        x_ref, gy_ref, wq_ref, wo_ref, w1_ref, w2_ref, small_ref,
+        x_in, gy_in, wq_ref, wo_ref, w1_ref, w2_ref, nv_ref, fb_ref, qb_ref, live_ref,
         own_g, own_1, own_2, out_ref, in_ref, tot_ref,
-        gg, g1, g2, gs, vec, bias, n1, r1, h1, qs, ks, vs, ps, os, x1, n2, r2, h2, slope, us, gfb,
+        x_ref, gy_ref, gg, g1, g2, gs, vec, bias, n1, r1, h1, qs, ks, vs, ps, os, x1, n2, r2, h2, slope, us, gfb,
         gx, gxb, gqkv, t_in, t_core, t_half, t_across, t_out,
         rs_in, rs_near, rs_sum, rs_far, sm,
         bsem_s, bsem_r, ysem_s, ysem_r, tsem_s, tsem_r, rsem_s, rsem_r, ssem_s, ssem_r,
@@ -568,7 +572,12 @@
             entry.start()
             pending.append(entry)
 
-        gs[mine] = small_ref[...]
+        gs[mine] = jnp.zeros(gs.shape[1:], low)
+        gs[mine, :vec_rows, :owned] = nv_ref[...].astype(low)
+        gs[mine, fc_row : fc_row + c_fc, : fb_ref.shape[1]] = fb_ref[...].astype(low)
+        for h in range(heads):
+            at = qv_row + 2 * h
+            gs[mine, at : at + 2, :c_qv] = qb_ref[h].astype(low)
         out_t = wo_ref[...].T.astype(low)
         gg[mine] = jnp.concatenate(
             [wq_ref[0].astype(low), wq_ref[1].astype(low), wq_ref[2].astype(low), out_t], axis=1
@@ -619,7 +628,7 @@
                         if s + 1 < far_n:
                             begin(ring(u, s + 1))
                         begin(cross(u, s))
-                    if s + 2 >= far_n and s + 1 < far_n or far_n == 2:
+                    if s == 1:
                         for u in after:
                             begin(ring(u, 1))
                 for u in after:
@@ -633,6 +642,15 @@
 
         step(1)
 
+        alive = [live_ref[i].astype(f32) for i in range(images)]
+        for i in range(images):
+            fill = jnp.zeros((padded - seqlen, width), low)
+            xi = x_in[:, i, :].astype(f32)
+            x_ref[i, :seqlen] = xi.astype(low)
+            x_ref[i, seqlen:] = fill
+            gi = gy_in[:, i, :].astype(f32) * alive[i]
+            gy_ref[i, :seqlen] = gi.astype(low)
+            gy_ref[i, seqlen:] = fill
         for i in range(images):
             xf = x_ref[i].astype(f32)
             center = xf - jnp.mean(xf, axis=-1, keepdims=True)
@@ -651,24 +669,32 @@
             first = jnp.dot(rows_d, pick, preferred_element_type=f32)
             source = lax.broadcasted_iota(jnp.int32, (lanes, hidden), 0)
             target = lax.broadcasted_iota(jnp.int32, (lanes, hidden), 1)
-            at = lax.div(source, c_fc) * (c_fc * fsdp) + d * c_fc + lax.rem(source, c_fc)
-            pick = ((target == at) & (source * fsdp < hidden)).astype(f32).astype(low)
+            pick = (lax.div(target, HD) == source).astype(f32).astype(low)
             second = jnp.dot(rows_d, pick, preferred_element_type=f32)
+            row = lax.broadcasted_iota(jnp.int32, (small_rows, hidden), 0) - fc_row
+            target = lax.broadcasted_iota(jnp.int32, (small_rows, hidden), 1)
+            keep = (row >= 0) & (row < c_fc) & (lax.rem(target, HD) == d * c_fc + row)
+            second = jnp.sum(jnp.where(keep, second, 0.0), axis=0, keepdims=True)
             source = lax.broadcasted_iota(jnp.int32, (lanes, wide), 0)
             target = lax.broadcasted_iota(jnp.int32, (lanes, wide), 1)
-            at = lax.div(source, c_qv) * (c_qv * fsdp) + d * c_qv + lax.rem(source, c_qv)
-            at = jnp.where(at < feat, at, at + feat)
-            pick = ((target == at) & (source < n_qv)).astype(f32).astype(low)
-            third = jnp.dot(rows_d, pick, preferred_element_type=f32)
+            pick = ((lax.rem(target, HD) == d * c_qv + source) & (source < c_qv)).astype(f32)
+            third = jnp.dot(rows_d, pick.astype(low), preferred_element_type=f32)
+            row = lax.broadcasted_iota(jnp.int32, (small_rows, wide), 0) - qv_row
+            target = lax.broadcasted_iota(jnp.int32, (small_rows, wide), 1)
+            group = lax.rem(row, 2) * (2 * heads) + lax.div(row, 2)
+            keep = (row >= 0) & (row < 2 * heads) & (lax.div(target, HD) == group)
+            third = jnp.sum(jnp.where(keep, third, 0.0), axis=0, keepdims=True)
             return (carry[0] + first, carry[1] + second, carry[2] + third)
 
-        small_rows = small_ref.shape[0]
-        start = tuple(jnp.zeros((small_rows, w), f32) for w in (width, hidden, wide))
-        spread_v, spread_h, spread_q = lax.fori_loop(0, fsdp, spread, start)
+        start = (
+            jnp.zeros((small_rows, width), f32),
+            jnp.zeros((1, hidden), f32),
+            jnp.zeros((1, wide), f32),
+        )
+        spread_v, bias_f, spread_q = lax.fori_loop(0, fsdp, spread, start)
         vec[...] = spread_v
         gain1, shift1, gain2, shift2, bias_o, bias_2 = (vec[r : r + 1] for r in range(6))
-        bias_f = spread_h[6:7]
-        bias[...] = spread_q[7:8]
+        bias[...] = spread_q
         for i in range(images):
             h1[i] = (n1[i] * gain1 + shift1).astype(low)
         cross_wait(1)
@@ -790,25 +816,10 @@
             phi = 0.5 * (1.0 + lax.erf(f * sqrt_half))
             us[i] = (f * phi).astype(low)
             slope[i] = phi + f * jnp.exp(-0.5 * f * f) * inv_root
-        cross_wait(5)
-        cross_wait(6)
-        two, mlp = [], []
-        gf_sum = None
-        row2 = row3 = None
-
-        def plus(a, b):
-            return b if a is None else a + b
-
-        for i in range(images):
-            gf = nn(gy_ref[i], flat(g2)) * slope[i]
-            gfb[i] = gf.astype(low)
-            gf_sum = plus(gf_sum, jnp.sum(gf, axis=0, keepdims=True))
-            t_in[1, i] = nt(gfb[i], flat(g1)).astype(low)
-            two.append(total(1, i))
-            next(two[i])
-
-        def scatter_y(p):
-            for j in list(range(1, far_n)) + [0]:
+        onward = tuple(range(1, far_n))
+
+        def scatter_y(p, steps):
+            for j in steps:
                 begin(copy(rs_in.at[p, 2 * ahead(j) + (1 - near)], rs_near.at[p, j],
                            rsem_s.at[p, j], rsem_r.at[p, j], twin))
 
@@ -834,12 +845,29 @@
         def blocks(grad):
             return grad.astype(low).reshape(fsdp, owned, grad.shape[1])
 
-        for i in range(images):
+        rs_in[0] = blocks(tn(flat(gy_ref), flat(us)))
+        cross_wait(5)
+        scatter_y(0, onward)
+        cross_wait(6)
+        two, mlp = [], []
+        gf_sum = None
+        row2 = row3 = None
+
+        def plus(a, b):
+            return b if a is None else a + b
+
+        for i in range(images):
+            gf = nn(gy_ref[i], flat(g2)) * slope[i]
+            gfb[i] = gf.astype(low)
+            gf_sum = plus(gf_sum, jnp.sum(gf, axis=0, keepdims=True))
+            t_in[1, i] = nt(gfb[i], flat(g1)).astype(low)
+            two.append(total(1, i))
             next(two[i])
-        rs_in[0] = blocks(tn(flat(gy_ref), flat(us)))
+
+        for i in range(images):
+            next(two[i])
         rs_in[1] = blocks(tn(flat(h2), flat(gfb)))
-        scatter_y(0)
-        scatter_y(1)
+        scatter_y(1, onward)
         for i in range(images):
             t_in[2, i] = nt(us[i], flat(g2)).astype(low)
         for i in range(images):
@@ -927,7 +955,9 @@
             reduce_step()
         for i in range(images):
             next(one[i])
-        scatter_y(2)
+        scatter_y(2, onward)
+        for p in range(3):
+            scatter_y(p, (0,))
         shared = lax.broadcasted_iota(jnp.int32, (8, width), 0) < 6
 
         def small_flow():
@@ -980,7 +1010,10 @@
             for _ in entry:
                 pass
         for i in range(images):
-            out_ref[i] = (x1[i] + t_out[2, i].astype(f32) + bias_2).astype(low)
+            x1[i] = x1[i] + t_out[2, i].astype(f32) + bias_2
+        out_ref[...] = jnp.stack(
+            [x1[i, :seqlen] * alive[i] for i in range(images)], axis=1
+        ).astype(low)
         for j in range(1, far_n):
             scatter_z(2, j)
         next(tiny)
@@ -989,11 +1022,12 @@
                 pass
             e = t_out[3, i].astype(f32) * gain1
             unit = n1[i]
-            in_ref[i] = gx[i] + r1[i] * (
+            grad_in = gx[i] + r1[i] * (
                 e
                 - jnp.mean(e, axis=-1, keepdims=True)
                 - unit * jnp.mean(e * unit, axis=-1, keepdims=True)
             )
+            in_ref[:, i, :] = grad_in[:seqlen]
         scatter_end(2, own_g)
         for entry in pending:
             entry.wait_send()
@@ -1003,8 +1037,8 @@
         shape((owned, combined), f32),
         shape((owned, hidden), f32),
         shape((owned, hidden), f32),
-        shape((images, padded, width), low),
-        shape((images, padded, width), f32),
+        shape((seqlen, images, width), low),
+        shape((seqlen, images, width), f32),
         shape((8, width), f32),
     )
     span = feat + HD
@@ -1017,11 +1051,12 @@
     xs = max(across_n - 1, 1)
     dma = pltpu.SemaphoreType.DMA
     scratch = [
+        vm(sp + (width,), low), vm(sp + (width,), low),
         vm((fsdp, owned, combined), low),
         vm((fsdp, owned, hidden), low),
         vm((fsdp, owned, hidden), low),
-        vm((fsdp,) + args[6].shape, low),
-        vm((args[6].shape[0], width), f32),
+        vm((fsdp, small_rows, lanes), low),
+        vm((small_rows, width), f32),
         vm((1, wide), f32),
         vm(sp + (width,), f32), vm(sp + (1,), f32), vm(sp + (width,), low),
         vm(sp + (span,), low), vm(sp + (span,), low), vm(sp + (span,), low),
@@ -1049,45 +1084,119 @@
     return pl.pallas_call(
         kernel,
         out_shape=outs,
-        in_specs=[space] * len(args),
+        in_specs=[space] * (len(args) - 1) + [pl.BlockSpec(memory_space=pltpu.SMEM)],
         out_specs=tuple([space] * len(outs)),
         scratch_shapes=scratch,
         compiler_params=pltpu.CompilerParams(
-            collective_id=1, has_side_effects=True, vmem_limit_bytes=60 * 1024 * 1024
+            collective_id=1, has_side_effects=True, vmem_limit_bytes=46 * 1024 * 1024
         ),
         name="fused_layer",
     )(*args)
 
 
-def update(own, params, moments):
-    count = len(own)
+def update(own_g, own_1, own_2, sums, out_rows, in_rows, params, moments):
+    f32 = jnp.float32
+    feat = params[0].shape[2]
+    owned = params[0].shape[1]
+    width = sums.shape[1]
+    heads, _, c_qv = params[4].shape
+    c_fc, r_fc = params[5].shape
+    vec_rows = params[6].shape[0]
 
     def kernel(*refs):
-        g_in, p_in, m_in = refs[:count], refs[count : 2 * count], refs[2 * count : 3 * count]
-        p_out, m_out = refs[3 * count : 4 * count], refs[4 * count : 5 * count]
-        for g, p, m, np_, nm in zip(g_in, p_in, m_in, p_out, m_out):
-            grad, param = g[...], p[...]
-            first = 0.9 * m[0] + 0.1 * grad
-            second = 0.999 * m[1] + 0.001 * grad * grad
-            np_[...] = param - 0.004 * (
+        g_ref, g1_ref, g2_ref, sum_ref = refs[:4]
+        rows_in, p_in, m_in = refs[4:6], refs[6:13], refs[13:20]
+        g_out, p_out, m_out, rows_out = refs[20:27], refs[27:34], refs[34:41], refs[41:43]
+        sems = refs[43]
+        moves = [
+            pltpu.make_async_copy(rows_in[k], rows_out[k], sems.at[k]) for k in range(2)
+        ]
+        for move in moves:
+            move.start()
+        mine = lax.axis_index("fsdp")
+
+        def advance(param, one, two, grad):
+            first = 0.9 * one + 0.1 * grad
+            second = 0.999 * two + 0.001 * grad * grad
+            fresh = param - 0.004 * (
                 first / corr_one / (jnp.sqrt(second / corr_two) + 1e-08) + 0.05 * param
             )
-            nm[0] = first
-            nm[1] = second
+            return fresh, first, second
+
+        for c in range(3):
+            grad = g_ref[:, c * feat : (c + 1) * feat]
+            g_out[0][c] = grad
+            p_out[0][c], m_out[0][0, c], m_out[0][1, c] = advance(
+                p_in[0][c], m_in[0][0, c], m_in[0][1, c], grad
+            )
+        for k, grad in ((1, g_ref[:, 3 * feat :].T), (2, g1_ref[...]), (3, g2_ref[...])):
+            g_out[k][...] = grad
+            p_out[k][...], m_out[k][0], m_out[k][1] = advance(
+                p_in[k][...], m_in[k][0], m_in[k][1], grad
+            )
+
+        def pick(rows, cols, values, row_of_lane, lane_base, step):
+            count = values.shape[1]
+            lane = lax.broadcasted_iota(jnp.int32, (rows, count), 1)
+            mask = row_of_lane(lane, lax.broadcasted_iota(jnp.int32, (rows, count), 0))
+            spread = jnp.where(mask, jnp.broadcast_to(values, (rows, count)), 0.0)
+            lane = lax.broadcasted_iota(jnp.int32, (count, 128), 0)
+            place = lax.broadcasted_iota(jnp.int32, (count, 128), 1)
+            chosen = (step(lane, place)).astype(f32)
+            return jnp.dot(
+                spread, chosen, precision=lax.Precision.HIGHEST, preferred_element_type=f32
+            )
+
+        hidden = sum_ref[vec_rows : vec_rows + 1]
+        grad = pick(
+            c_fc, r_fc, hidden,
+            lambda l, r: lax.rem(l, HD) == mine * c_fc + r, None,
+            lambda l, p: lax.div(l, HD) == p,
+        )[:, :r_fc]
+        g_out[5][...] = grad
+        p_out[5][...], m_out[5][0], m_out[5][1] = advance(
+            p_in[5][...], m_in[5][0], m_in[5][1], grad
+        )
+        triple = sum_ref[vec_rows + 1 : vec_rows + 2]
+        grads = pick(
+            8, c_qv, triple,
+            lambda l, r: lax.div(l, HD) == lax.rem(r, 2) * (2 * heads) + lax.div(r, 2), None,
+            lambda l, p: (lax.rem(l, HD) == mine * c_qv + p) & (p < c_qv),
+        )
+        for h in range(heads):
+            grad = grads[2 * h : 2 * h + 2, :c_qv]
+            g_out[4][h] = grad
+            p_out[4][h], m_out[4][0, h], m_out[4][1, h] = advance(
+                p_in[4][h], m_in[4][0, h], m_in[4][1, h], grad
+            )
+        lane = lax.broadcasted_iota(jnp.int32, (width, 128), 0)
+        place = lax.broadcasted_iota(jnp.int32, (width, 128), 1)
+        chosen = ((lane == mine * owned + place) & (place < owned)).astype(f32)
+        grad = jnp.dot(
+            sum_ref[...], chosen, precision=lax.Precision.HIGHEST, preferred_element_type=f32
+        )[:vec_rows, :owned]
+        g_out[6][...] = grad
+        p_out[6][...], one, two = advance(p_in[6][...], m_in[6][:, 0], m_in[6][:, 1], grad)
+        m_out[6][:, 0] = one
+        m_out[6][:, 1] = two
+        for move in moves:
+            move.wait()
 
     shape = jax.ShapeDtypeStruct
-    outs = [shape(p.shape, jnp.float32) for p in params]
-    outs += [shape(m.shape, jnp.float32) for m in moments]
+    outs = [shape(p.shape, f32) for p in params] * 2 + [shape(m.shape, f32) for m in moments]
+    outs += [shape(a.shape, a.dtype) for a in (out_rows, in_rows)]
     space = pl.BlockSpec(memory_space=pltpu.VMEM)
+    spaces = [space] * 21 + [pl.BlockSpec(memory_space=pl.ANY)] * 2
     result = pl.pallas_call(
         kernel,
         out_shape=tuple(outs),
-        in_specs=[space] * (3 * count),
-        out_specs=tuple([space] * len(outs)),
-        compiler_params=pltpu.CompilerParams(vmem_limit_bytes=40 * 1024 * 1024),
+        in_specs=[space] * 20,
+        out_specs=tuple(spaces),
+        scratch_shapes=[pltpu.SemaphoreType.DMA((2,))],
+        compiler_params=pltpu.CompilerParams(vmem_limit_bytes=24 * 1024 * 1024),
         name="update",
-    )(*own, *params, *moments)
-    return result[:count], result[count:]
+    )(own_g, own_1, own_2, sums, out_rows, in_rows, *params, *moments)
+    return result[:7], result[7:14], result[14:21], result[21:]
 
 
 def on_device(fsdp, tensor, *args):
@@ -1107,59 +1216,36 @@
     fsdp, tensor, block_input, output_grad, live_images, w_qkv, w_out, w_fc1, w_fc2, qv_bias,
     fc1_bias, norm_vec, mom_qkv, mom_out, mom_fc1, mom_fc2, mom_qvb, mom_fc1b, mom_vec,
 ):
-    low, f32 = jnp.bfloat16, jnp.float32
     images, seqlen, width = block_input.shape
     owned, _, feat = w_qkv.shape
     hidden = w_fc1.shape[1]
-    n_qv, n_fc = qv_bias.size, fc1_bias.size
-    vec_rows = norm_vec.shape[0]
-    lanes = -(-max(owned, n_qv, n_fc) // 128) * 128
-    padded = -(-seqlen // 16) * 16
-    live = live_images.astype(low)[:, None, None]
-    edge = ((0, 0), (0, padded - seqlen), (0, 0))
-    x_pad = jnp.pad(block_input, edge)
-    gy_pad = jnp.pad(output_grad * live, edge)
-    small = jnp.concatenate(
-        [
-            row_of(norm_vec, lanes),
-            row_of(fc1_bias.reshape(1, n_fc), lanes),
-            row_of(qv_bias.reshape(1, n_qv), lanes),
-            jnp.zeros((16 - vec_rows - 2, lanes), f32),
-        ]
-    ).astype(low)
-    dims = (images, seqlen, width, owned, feat, hidden, fc1_bias.shape[1], qv_bias.shape[2], n_qv)
+    x_t, gy_t = block_input.transpose(1, 0, 2), output_grad.transpose(1, 0, 2)
+    nv, fb, qb = norm_vec, fc1_bias.T, qv_bias.transpose(1, 0, 2)
+    dims = (images, seqlen, width, owned, feat, hidden, fc1_bias.shape[1], qv_bias.shape[2])
     wq, w2 = w_qkv.transpose(1, 0, 2), w_fc2.T
     own_g, own_1, own_2, out_rows, in_rows, sums = fused(
-        fsdp, tensor, dims, (x_pad, gy_pad, wq, w_out, w_fc1, w2, small)
-    )
-    block_output = out_rows[:, :seqlen] * live
-    input_grad = in_rows[:, :seqlen]
-    g_qkv = jnp.stack([own_g[:, c * feat : (c + 1) * feat] for c in range(3)])
-    g_out = own_g[:, 3 * feat :].T
-    news, moms = update(
-        (g_qkv, g_out, own_1, own_2),
-        (wq, w_out, w_fc1, w2),
-        (mom_qkv.transpose(0, 2, 1, 3), mom_out, mom_fc1, mom_fc2.transpose(0, 2, 1)),
-    )
-    mine = lax.axis_index("fsdp")
-    g_vec = lax.dynamic_slice(sums, (0, mine * owned), (vec_rows, owned))
-    r_fc, c_fc = fc1_bias.shape
-    g_fc1b = lax.dynamic_slice(
-        sums[vec_rows].reshape(r_fc, fsdp * c_fc), (0, mine * c_fc), (r_fc, c_fc)
-    )
-    k_qv, r_qv, c_qv = qv_bias.shape
-    row = sums[vec_rows + 1]
-    pair = jnp.stack([row[:feat], row[2 * feat : 3 * feat]]).reshape(k_qv, r_qv, fsdp * c_qv)
-    g_qvb = lax.dynamic_slice(pair, (0, 0, mine * c_qv), (k_qv, r_qv, c_qv))
-    qvb = adamw(qv_bias, g_qvb, mom_qvb)
-    fcb = adamw(fc1_bias, g_fc1b, mom_fc1b)
-    nvec = adamw(norm_vec, g_vec, mom_vec)
+        fsdp, tensor, dims, (x_t, gy_t, wq, w_out, w_fc1, w2, nv, fb, qb, live_images)
+    )
+    grads, news, moms, flows = update(
+        own_g, own_1, own_2, sums, out_rows, in_rows,
+        (wq, w_out, w_fc1, w2, qb, fb, nv),
+        (
+            mom_qkv.transpose(0, 2, 1, 3), mom_out, mom_fc1, mom_fc2.transpose(0, 2, 1),
+            mom_qvb.transpose(0, 2, 1, 3), mom_fc1b.transpose(0, 2, 1), mom_vec.transpose(1, 0, 2),
+        ),
+    )
+
+    def back(a):
+        return (
+            a[0].transpose(1, 0, 2), a[1], a[2], a[3].T, a[4].transpose(1, 0, 2), a[5].T, a[6],
+        )
+
     return (
-        block_output, input_grad,
-        g_qkv.transpose(1, 0, 2), g_out, own_1, own_2.T, g_qvb, g_fc1b, g_vec,
-        news[0].transpose(1, 0, 2), news[1], news[2], news[3].T, qvb[0], fcb[0], nvec[0],
-        moms[0].transpose(0, 2, 1, 3), moms[1], moms[2], moms[3].transpose(0, 2, 1),
-        qvb[1], fcb[1], nvec[1],
+        tuple(a.transpose(1, 0, 2) for a in flows) + back(grads) + back(news)
+        + (
+            moms[0].transpose(0, 2, 1, 3), moms[1], moms[2], moms[3].transpose(0, 2, 1),
+            moms[4].transpose(0, 2, 1, 3), moms[5].transpose(0, 2, 1), moms[6].transpose(1, 0, 2),
+        )
     )
 
 

time: 149 us -> 130 us (0.87)
  local copies, waits for them, and re-layouts: 21 us -> 8.66 us
  other arithmetic: 8.14 us -> 0 us
  Pallas kernels: 118 us -> 120 us
    another operation x10 -> x0, other arithmetic: 3.99 us -> none  [the longest x6 3.21 us: adamw(): return (fresh, jnp.stack([first, second]))]
    slice x4 -> x0, local copies, waits for them, and re-layouts: 2.9 us -> none  [the longest x1 1.29 us: fused_step(): row[:feat]]
    another operation x7 -> x0, local copies, waits for them, and re-layouts: 2.35 us -> none  [the longest x2 2.09 us: fused_step(): jnp.stack([row[:feat], row[2 * feat:3 * feat]])]
    mul x3 -> x0, other arithmetic: 2.11 us -> none  [the longest x1 1.29 us: fused_step(): block_output = out_rows[:, :seqlen] * live]
    pallas_call x1 -> x0, local copies, waits for them, and re-layouts: 1.88 us -> none  [fused(): pl.pallas_call(kernel, out_shape=outs, in_specs=[space] * len(args), out_...]
    pad x2 -> x0, local copies, waits for them, and re-layouts: 1.77 us -> none  [the longest x1 0.89 us: fused_step(): gy_pad = jnp.pad(output_grad * live, edge)]
    unnamed x61 -> x34, local copies, waits for them, and re-layouts: 10.2 us -> 8.66 us
    transpose x1 -> x0, local copies, waits for them, and re-layouts: 1.54 us -> none  [fused_step(): g_out = own_g[:, 3 * feat:].T]
where the time goes in v2:
time: 130 us; the launch traced here: 129 us
  Pallas kernels  120 us (92%)
  local copies, waits for them, and re-layouts  8.66 us (7%)
    pallas_call x1, Pallas kernels, fused(): pl.pallas_call(kernel, out_shape=outs, in_specs=[space] * (len(args) - 1)...  115 us
    unnamed x34, local copies, waits for them, and re-layouts  8.66 us
    pallas_call x1, Pallas kernels, update(): pl.pallas_call(kernel, out_shape=tuple(outs), in_specs=[space] * 20, out_...  5.12 us

profile of v2, /device:TPU:0, one launch (start us, length us, event | category | flops | bytes accessed | tf_op | source)
XLA Modules:
  0.0 129.3 jit_solution(4221695264608450948)
XLA Ops:
  0.7 0.0 copy-start.15
  0.7 0.0 copy-start.13
  0.7 0.0 copy-start.14
  0.7 0.0 copy-start
  0.7 1.0 copy-done
  1.7 0.0 copy-start.1
  1.7 1.0 copy-done.1
  2.6 1.0 copy-done.2
  3.6 1.1 copy-done.3
  4.7 1.1 copy-done.4
  5.7 0.9 copy-done.8
  6.6 0.7 copy-done.10
  7.3 0.7 copy-done.11
  8.0 0.7 copy-done.12
  8.7 0.7 copy-done.16
  9.4 114.6 %fused_layer.1 = (f32[96,768]{1,0:T(8,128)S(1)}, f32[96,768]{1,0:T(8,128)S(1)}, f32[96,768]{1,0:T(8,128)S(1)}, bf16[197,2,768]{2,1,0:T(2,128)(2,1)S(1)}, f32[197...) custom-call(bf16[197,2,768]{2,1,0:T(2,128)(2,1)S(1)} %bitcast.30, bf16[197,2,768]{2,1,0:T(2,128)(2,1)S(1)} %bitcast.31, ...), custom_call_target="tpu_custom_call" | custom-call | tf_op jit(solution)/shard_map/fused_layer/pallas_call | solution.py:1084
  124.0 0.0 copy-done.15
  124.0 0.0 copy-done.13
  124.0 0.0 copy-done.14
  124.0 0.0 copy-done.5
  124.0 0.0 copy-done.6
  124.0 0.0 copy-done.7
  124.0 0.0 copy-done.9
  124.0 5.1 %update.1 = (f32[3,96,192]{2,1,0:T(8,128)}, f32[192,96]{1,0:T(8,128)}, f32[96,768]{1,0:T(8,128)}, f32[96,768]{1,0:T(8,128)}, f32[3,2,8]{2,1,0:T(2,128)}, /*index...) custom-call(f32[96,768]{1,0:T(8,128)S(1)} %get-tuple-element.52.refs, ...), custom_call_target="tpu_custom_call" | custom-call | tf_op jit(solution)/shard_map/update/pallas_call | solution.py:1190
  (12 shorter events, 0.0 us)
Async XLA Ops:
  0.7 123.3 %copy-start.15 = (f32[2,6,96]{2,0,1:T(2,128)S(1)}, f32[2,6,96]{2,0,1:T(2,128)}, u32[]{:S(2)}) copy-start(f32[2,6,96]{2,0,1:T(2,128)} %param.33) | copy-start | bytes 13828
  0.7 123.3 %copy-start.13 = (f32[2,12,8]{1,2,0:T(8,128)S(1)}, f32[2,12,8]{1,2,0:T(8,128)}, u32[]{:S(2)}) copy-start(f32[2,12,8]{1,2,0:T(8,128)} %param.32) | copy-start | bytes 2308
  0.7 123.3 %copy-start.14 = (f32[2,2,3,8]{3,1,2,0:T(2,128)S(1)}, f32[2,2,3,8]{3,1,2,0:T(2,128)}, u32[]{:S(2)}) copy-start(f32[2,2,3,8]{3,1,2,0:T(2,128)} %param.31) | copy-start | bytes 1156
  0.7 1.0 copy-start
  1.7 1.0 copy-start.1
  2.6 1.0 copy-start.2
  3.6 1.1 copy-start.3
  4.7 1.1 copy-start.4
  5.7 0.9 copy-start.8
  6.6 0.7 copy-start.10
  7.3 0.7 copy-start.11
  8.0 0.7 copy-start.12
  8.7 0.7 copy-start.16
  9.3 114.6 %copy-start.5 = (f32[2,96,3,192]{3,1,2,0:T(8,128)S(1)}, f32[2,96,3,192]{3,1,2,0:T(8,128)}, u32[]{:S(2)}) copy-start(f32[2,96,3,192]{3,1,2,0:T(8,128)} %param.27) | copy-start | bytes 1327108
  9.4 114.7 %copy-start.6 = (f32[2,96,768]{2,1,0:T(8,128)S(1)}, f32[2,96,768]{2,1,0:T(8,128)}, u32[]{:S(2)}) copy-start(f32[2,96,768]{2,1,0:T(8,128)} %refs_15_.1) | copy-start | bytes 1769476
  9.4 114.7 %copy-start.7 = (f32[2,768,96]{1,2,0:T(8,128)S(1)}, f32[2,768,96]{1,2,0:T(8,128)}, u32[]{:S(2)}) copy-start(f32[2,768,96]{1,2,0:T(8,128)} %param.30) | copy-start | bytes 1769476
  9.4 114.7 %copy-start.9 = (f32[2,192,96]{2,1,0:T(8,128)S(1)}, f32[2,192,96]{2,1,0:T(8,128)}, u32[]{:S(2)}) copy-start(f32[2,192,96]{2,1,0:T(8,128)} %refs_14_.1) | copy-start | bytes 442372
